TPU v7x, 32 devices: a whole 2x2x4 slice. The times are simulated.
32 devices in a mesh: member: 4 (over y, x), group: 8 (over z, core).
Axes of the slice: x: 2, y: 2, z: 4, core: 2. Of those that a mesh axis runs over, the one named last changes fastest.
Arguments:
- agg_one: bfloat16 [16384, 768], P(('member', 'group')), may hold values from -6 to 6
- agg_two: bfloat16 [16384, 768], P(('member', 'group')), may hold values from -6 to 6
- grad_out: bfloat16 [16384, 768], P(('member', 'group')), may hold values from -6 to 6
- hop_one_weight: bfloat16 [768, 768], replicated, may hold values from -0.21875 to 0.21875
- hop_two_weight: bfloat16 [768, 768], replicated, may hold values from -0.21875 to 0.21875
- block_values: bfloat16 [768, 256, 256], P(('member', 'group')), may hold values from 0 to 0.046875
- src_slot: int32 [32, 24], P(('member', 'group')), may hold values from 0 to 13, as said below
- dst_block: int32 [32, 24], P(('member', 'group')), may hold values from 0 to 1
- block_count: int32 [32], P(('member', 'group')), may hold values from 9 to 24, as said below
- send_member: int32 [32, 4, 1], P(('member', 'group')), may hold values from 0 to 1, as said below
- send_group: int32 [32, 8], P(('member', 'group')), may hold values from 0 to 1, as said below
Outputs:
- grad_emb: bfloat16 [16384, 768], P(('member', 'group'))
- grad_w_one: float32 [768, 768], replicated
- grad_w_two: float32 [768, 768], replicated
Inputs may be any that keep to these rules, and one draw needn't show every extreme that they name: `send_member`: for device d, entry [d, p, 0] is the label block of d, counted within d, sent to the device of member index p in d's group; one for every p. `send_group`: entry [d, h] is the label block of d, counted within d, sent to the device of group h with d's member index; one for every h. The first block_count[d] slots of device d are live, the rest hold 0 in src_slot and dst_block and are not read; some device has all 24 slots live. `src_slot`: For device d of group g, slot j < 8 - 1 holds 2 + 4 + ((g + 1 + j) % 8); every later slot holds a value under 2 + 4.
All inputs are finite; a program needn't handle non-finite values.
Results may differ from a plain program's by a relative error of at most 0.0065.
Values may be sent and summed in bfloat16 or wider, within the bound.
No kernel may reach another device: no remote copies, remote signals or barrier semaphores. Data moves between devices by JAX's collectives and lax.ppermute only.
A program may use at most 128 MiB of HBM per device.

v0:
```python
import functools

import jax
import jax.numpy as jnp
from jax import lax
from jax.experimental import pallas as pl
from jax.experimental.pallas import tpu as pltpu
from jax.sharding import PartitionSpec as P


F32 = jnp.float32
BF16 = jnp.bfloat16
VMEM = pl.BlockSpec(memory_space=pltpu.VMEM)
SMEM = pl.BlockSpec(memory_space=pltpu.SMEM)
ANY = pl.BlockSpec(memory_space=pl.ANY)
LIMIT = 48 << 20
PAIR = 2


def silu_slope(value):
    sig = jax.nn.sigmoid(value)
    return sig * (1.0 + value * (1.0 - sig))


def turned_dot(values, rows):
    return lax.dot_general(values, rows, (((0,), (0,)), ((), ())), preferred_element_type=F32)


def times_transpose(left, weight):
    return lax.dot_general(left, weight, (((1,), (1,)), ((), ())), preferred_element_type=F32)


def start_sends(back, send_group, send_member, group_outs, member_outs, sems, rows):
    members, capacity = send_member.shape[1], send_member.shape[2]
    own_group, own_member = lax.axis_index("group"), lax.axis_index("member")
    copies = []

    def send(block, out):
        source = back.at[pl.ds(pl.multiple_of(block * rows, rows), rows), :]
        copies.append(pltpu.make_async_copy(source, out, sems.at[len(copies)]))
        copies[-1].start()

    for place, out in enumerate(group_outs):
        send(send_group[0, own_group ^ (place + 1)], out)
    for place, out in enumerate(member_outs):
        shift, which = 1 + place // capacity, place % capacity
        send(send_member[0, lax.rem(own_member + shift, members), which], out)
    return copies


def first_kernel(rows, cross, send_group, send_member, agg, weight, grad, pull_out, back_out, *rest):
    *outs, sems = rest
    for start in range(0, agg.shape[0], rows):
        part = pl.ds(start, rows)
        lift = jnp.dot(agg[part, :], weight[...], preferred_element_type=F32)
        pull = (grad[part, :].astype(F32) * silu_slope(lift)).astype(BF16)
        pull_out[part, :] = pull
        back_out[part, :] = times_transpose(pull, weight[...]).astype(BF16)
    for copy in start_sends(back_out, send_group, send_member, outs[:cross], outs[cross:], sems, rows):
        copy.wait()


def sweep_kernel(rows, cross, src_slot, dst_block, block_count, send_member, back, base, values, *rest):
    *received, total, pool, sems = rest
    members, capacity = send_member.shape[1], send_member.shape[2]
    local = back.shape[0] // rows
    own = lax.axis_index("member")
    copies = []

    def fill(source, slot):
        copies.append(pltpu.make_async_copy(source, pool.at[slot], sems.at[len(copies)]))
        copies[-1].start()

    for block in range(local):
        fill(back.at[pl.ds(block * rows, rows), :], block)
    for which in range(capacity):
        block = send_member[0, own, which]
        fill(back.at[pl.ds(pl.multiple_of(block * rows, rows), rows), :], local + own * capacity + which)
    for place, source in enumerate(received):
        shift, which = 1 + place // capacity, place % capacity
        peer = lax.rem(own + (members - shift), members)
        fill(source, local + peer * capacity + which)
    total[...] = base[...].astype(F32).reshape(total.shape)
    for copy in copies:
        copy.wait()

    def step(slot, carry):
        total[dst_block[0, slot]] += turned_dot(values[slot], pool[src_slot[0, slot]])
        return carry

    lax.fori_loop(cross, block_count[0], step, 0)


def is_inner(groups):
    chip = lax.axis_index("group") // PAIR
    return (chip > 0) & (chip < groups // PAIR - 1)


def fetch_cross(rows, groups, far_table, received, blocks, values, held, sems):
    own = lax.axis_index("group")
    loads = []

    def load(source, to):
        copy = pltpu.make_async_copy(source, to, sems.at[len(loads)])
        loads.append(copy)
        return copy

    for place, sources in enumerate(received):
        slot = lax.rem((own ^ (place + 1)) + (groups - 1 - own), groups)
        load(values.at[slot], held.at[place]).start()
        if len(sources) == 1:
            load(sources[0], blocks.at[place]).start()
            continue
        inner, outer = sources
        if inner.shape[0] != rows:
            picked = pl.multiple_of(far_table[0, own] * rows, rows)
            inner = inner.at[pl.ds(picked, rows), :]
        near = pltpu.make_async_copy(inner, blocks.at[place], sems.at[len(loads)])
        copy = load(outer, blocks.at[place])
        deep = is_inner(groups)

        @pl.when(deep)
        def _():
            near.start()

        @pl.when(jnp.logical_not(deep))
        def _():
            copy.start()

    return loads


def add_cross(groups, total, dst_block, held, blocks, loads):
    own = lax.axis_index("group")
    for place in range(groups - 1):
        slot = lax.rem((own ^ (place + 1)) + (groups - 1 - own), groups)
        loads[2 * place].wait()
        loads[2 * place + 1].wait()
        total[dst_block[0, slot]] += turned_dot(held[place], blocks[place])


def split_received(plan, refs):
    received = []
    for count in plan:
        received.append(refs[:count])
        refs = refs[count:]
    return received, refs


def relay_kernel(rows, far_table, raw, *rest):
    *outs, sems = rest
    own = lax.axis_index("group")
    copies = []
    for i, (peer, out) in enumerate(zip((1, 2, 3), outs)):
        block = far_table[0, own ^ peer]
        source = raw.at[pl.ds(pl.multiple_of(block * rows, rows), rows), :]
        copies.append(pltpu.make_async_copy(source, out, sems.at[i]))
        copies[-1].start()
    for copy in copies:
        copy.wait()


def middle_kernel(
    rows, plan, send_group, send_member, dst_block, far_table, base, slope, weight, values, after, *rest
):
    received, rest = split_received(plan, rest)
    cross = len(plan)
    carry_out, pull_out, back_out, *outs, held, blocks, sems, send_sems = rest
    loads = fetch_cross(rows, cross + 1, far_table, received, blocks, values, held, sems)
    carry_out[...] = base[...]
    add_cross(cross + 1, carry_out, dst_block, held, blocks, loads)
    for block in range(carry_out.shape[0]):
        part = pl.ds(block * rows, rows)
        pull = (carry_out[block] * slope[part, :]).astype(BF16)
        pull_out[part, :] = pull
        back_out[part, :] = times_transpose(pull, weight[...]).astype(BF16)
    for copy in start_sends(back_out, send_group, send_member, outs[:cross], outs[cross:], send_sems, rows):
        copy.wait()


def last_kernel(rows, plan, dst_block, far_table, base, values, after, *rest):
    received, (out, total, held, blocks, sems) = split_received(plan, rest)
    loads = fetch_cross(rows, len(plan) + 1, far_table, received, blocks, values, held, sems)
    total[...] = base[...]
    add_cross(len(plan) + 1, total, dst_block, held, blocks, loads)
    out[...] = total[...].reshape(out.shape).astype(BF16)


def params():
    return pltpu.CompilerParams(vmem_limit_bytes=LIMIT)


def send_shapes(rows, width, count):
    return [jax.ShapeDtypeStruct((rows, width), BF16)] * count


def relayed(groups):
    return groups == 4 * PAIR


def group_exchange(rows, back, group_sends, far_table):
    groups = lax.axis_size("group")
    line = relayed(groups)

    def inner(g):
        return 0 < g // PAIR < groups // PAIR - 1

    def permute(block, peer, keep=lambda g: True):
        return lax.ppermute(block, "group", [(g, g ^ peer) for g in range(groups) if keep(g)])

    if not line:
        return [[permute(block, peer)] for peer, block in enumerate(group_sends, 1)]
    raw = permute(back, 6, inner)
    near = {peer: permute(group_sends[peer - 1], peer) for peer in (2, 3)}
    far = {peer: permute(group_sends[peer - 1], peer, lambda g: not inner(g)) for peer in (6, 7, 4, 5)}
    sibling = permute(group_sends[0], 1)
    to_sibling, to_same, to_cross = pl.pallas_call(
        functools.partial(relay_kernel, rows),
        out_shape=send_shapes(rows, back.shape[1], 3),
        in_specs=[SMEM, ANY],
        out_specs=[ANY] * 3,
        scratch_shapes=[pltpu.SemaphoreType.DMA((3,))],
        compiler_params=params(),
        name="relay_pick",
    )(far_table, raw)
    same = permute(to_same, 2, inner)
    cross = permute(to_cross, 3, inner)
    swapped = permute(to_sibling, 1, inner)
    return [
        [sibling],
        [near[2]],
        [near[3]],
        [far[4], same],
        [far[5], cross],
        [raw, far[6]],
        [swapped, far[7]],
    ]


def member_exchange(member_sends, capacity):
    members = lax.axis_size("member")
    return [
        lax.ppermute(block, "member", [(m, (m + 1 + place // capacity) % members) for m in range(members)])
        for place, block in enumerate(member_sends)
    ]


def stage_peers(axis, stride, size):
    total = lax.axis_size(axis)

    def moved(index, shift):
        place = index // stride % size
        return index + ((place + shift) % size - place) * stride

    perms = [[(i, moved(i, shift)) for i in range(total)] for shift in range(1, size)]
    return lax.axis_index(axis) // stride % size, perms


def weight_total(part):
    groups, members = lax.axis_size("group"), lax.axis_size("member")
    stages = [("group", 1, PAIR), ("member", 1, members), ("group", PAIR, groups // PAIR)]
    for axis, stride, size in stages:
        place, perms = stage_peers(axis, stride, size)
        pieces = part.reshape(size, part.shape[0] // size, part.shape[1])

        def piece(shift):
            return lax.dynamic_index_in_dim(pieces, (place + shift) % size, 0, keepdims=False)

        got = [
            lax.ppermute(piece(shift).astype(BF16), axis, perm) for shift, perm in enumerate(perms, 1)
        ]
        part = sum((block.astype(F32) for block in got), piece(0))
    part = part.astype(BF16)
    for axis, stride, size in reversed(stages):
        place, perms = stage_peers(axis, stride, size)
        whole = jnp.zeros((size,) + part.shape, BF16)
        whole = lax.dynamic_update_index_in_dim(whole, part, place, 0)
        for shift, perm in enumerate(perms, 1):
            block = lax.ppermute(part, axis, perm)
            whole = lax.dynamic_update_index_in_dim(whole, block, (place - shift) % size, 0)
        part = whole.reshape(size * part.shape[0], part.shape[1])
    return part.astype(F32)


def weight_part(aggregate, pulled):
    return lax.dot_general(aggregate, pulled, (((0,), (0,)), ((), ())), preferred_element_type=F32)


def body(
    agg_one,
    agg_two,
    grad_out,
    hop_one_weight,
    hop_two_weight,
    block_values,
    src_slot,
    dst_block,
    block_count,
    send_member,
    send_group,
):
    groups, members = lax.axis_size("group"), lax.axis_size("member")
    labels, width = agg_one.shape
    _, rows = block_values.shape[:2]
    local = labels // rows
    capacity = send_member.shape[2]
    cross = groups - 1
    peers = (members - 1) * capacity
    grad_scale = float(labels * members * groups) ** (-0.5)

    field = jax.ShapeDtypeStruct((labels, width), BF16)
    total = jax.ShapeDtypeStruct((local, rows, width), F32)
    sends = send_shapes(rows, width, cross + peers)
    send_sems = pltpu.SemaphoreType.DMA((cross + peers,))
    cross_scratch = [
        pltpu.VMEM((cross, rows, rows), BF16),
        pltpu.VMEM((cross, rows, width), BF16),
    ]

    def sweep(back, base, received):
        return pl.pallas_call(
            functools.partial(sweep_kernel, rows, cross),
            out_shape=total,
            in_specs=[SMEM, SMEM, SMEM, SMEM, ANY, VMEM, VMEM] + [ANY] * peers,
            out_specs=VMEM,
            scratch_shapes=[
                pltpu.VMEM((local + members * capacity, rows, width), BF16),
                pltpu.SemaphoreType.DMA((local + members * capacity,)),
            ],
            compiler_params=params(),
            name="sweep",
        )(src_slot, dst_block, block_count, send_member, back, base, block_values, *received)

    far_table = send_group
    if relayed(groups):
        far_table = lax.ppermute(send_group, "group", [(g, g ^ 6) for g in range(groups)])
    plan = [1, 1, 1, 2, 2, 2, 2] if relayed(groups) else [1] * cross

    pull_two, back_two, *outs = pl.pallas_call(
        functools.partial(first_kernel, rows, cross),
        out_shape=[field, field] + sends,
        in_specs=[SMEM, SMEM, VMEM, VMEM, VMEM],
        out_specs=[VMEM, VMEM] + [ANY] * (cross + peers),
        scratch_shapes=[send_sems],
        compiler_params=params(),
        name="first",
    )(send_group, send_member, agg_two, hop_two_weight, grad_out)
    from_group = group_exchange(rows, back_two, outs[:cross], far_table)
    from_member = member_exchange(outs[cross:], capacity)
    slope_one = silu_slope(jnp.dot(agg_one, hop_one_weight, preferred_element_type=F32))
    grad_w_two = weight_total(weight_part(agg_two, pull_two)) * grad_scale
    base_two = sweep(back_two, grad_out, from_member)

    carry, pull_one, back_one, *outs = pl.pallas_call(
        functools.partial(middle_kernel, rows, plan),
        out_shape=[total, field, field] + sends,
        in_specs=[SMEM] * 4 + [VMEM] * 3 + [ANY] * (2 + sum(plan)),
        out_specs=[VMEM, VMEM, VMEM] + [ANY] * (cross + peers),
        scratch_shapes=cross_scratch + [pltpu.SemaphoreType.DMA((2 * cross,)), send_sems],
        compiler_params=params(),
        name="middle",
    )(
        *(send_group, send_member, dst_block, far_table, base_two, slope_one),
        *(hop_one_weight, block_values, grad_w_two),
        *sum(from_group, []),
    )
    from_group = group_exchange(rows, back_one, outs[:cross], far_table)
    from_member = member_exchange(outs[cross:], capacity)
    grad_w_one = weight_total(weight_part(agg_one, pull_one)) * grad_scale
    base_one = sweep(back_one, carry, from_member)

    grad_emb = pl.pallas_call(
        functools.partial(last_kernel, rows, plan),
        out_shape=field,
        in_specs=[SMEM] * 2 + [VMEM] + [ANY] * (2 + sum(plan)),
        out_specs=VMEM,
        scratch_shapes=[pltpu.VMEM((local, rows, width), F32)]
        + cross_scratch
        + [pltpu.SemaphoreType.DMA((2 * cross,))],
        compiler_params=params(),
        name="last",
    )(dst_block, far_table, base_one, block_values, grad_w_one, *sum(from_group, []))
    return (grad_emb, grad_w_one, grad_w_two)


def solution(mesh):
    in_specs = (
        P(("member", "group"), None),
        P(("member", "group"), None),
        P(("member", "group"), None),
        P(),
        P(),
        P(("member", "group"), None, None),
        P(("member", "group"), None),
        P(("member", "group"), None),
        P(("member", "group")),
        P(("member", "group"), None, None),
        P(("member", "group"), None),
    )
    out_specs = (P(("member", "group"), None), P(), P())
    return jax.shard_map(body, mesh=mesh, in_specs=in_specs, out_specs=out_specs, check_vma=False)
```

profile of v0, /device:TPU:4, one launch (start us, length us, event | category | flops | bytes accessed | tf_op | source)
XLA Modules:
  0.0 285.3 jit_solution(17805897742826136875)
XLA Ops:
  2.1 5.7 %first.1 = (bf16[512,768]{1,0:T(8,128)(2,1)S(1)}, bf16[512,768]{1,0:T(8,128)(2,1)S(1)}, bf16[256,768]{1,0:T(8,128)(2,1)S(1)}, bf16[256,768]{1,0:T(8,128)(2,1)S(1...) custom-call(s32[1,8]{1,0:T(1,128)S(1)} %copy-done.8, ...), custom_call_target="tpu_custom_call" | custom-call | tf_op jit(solution)/shard_map/first/pallas_call | solution.py:339
  24.6 4.9 %collective-permute-done.5 = bf16[96,768]{1,0:T(8,128)(2,1)S(1)} collective-permute-done((bf16[96,768]{1,0:T(8,128)(2,1)}, bf16[96,768]{1,0:T(8,128)(2,1)S(1)}, u32[]{:S(2)}, u32[]{:S(2)}) %collective-permute-start.5) | collective-permute-done | bytes 147488 | tf_op jit(solution)/shard_map/ppermute | solution.py:270
  62.4 4.7 %collective-permute-done.15 = bf16[96,768]{1,0:T(8,128)(2,1)S(1)} collective-permute-done((bf16[96,768]{1,0:T(8,128)(2,1)}, bf16[96,768]{1,0:T(8,128)(2,1)S(1)}, u32[]{:S(2)}, u32[]{:S(2)}) %collective-permute-start.15) | collective-permute-done | bytes 147488 | tf_op jit(solution)/shard_map/ppermute | solution.py:279
  69.6 5.8 %collective-permute-done.2.rest_1_ = bf16[256,768]{1,0:T(8,128)(2,1)S(1)} collective-permute-done((bf16[256,768]{1,0:T(8,128)(2,1)}, bf16[256,768]{1,0:T(8,128)(2,1)S(1)}, u32[]{:S(2)}, u32[]{:S(2)}) %collective-permute-start.2) | collective-permute-done | bytes 393248 | tf_op jit(solution)/shard_map/ppermute | solution.py:243
  87.1 4.1 %sweep.2.base = f32[2,256,768]{2,1,0:T(8,128)S(1)} custom-call(s32[1,24]{1,0:T(1,128)S(1)} %copy-done.10, s32[1,24]{1,0:T(1,128)S(1)} %copy-done.7, s32[1]{0:T(128)S(6)} %copy.38.block_count, s32[1,4,1]{2,1,0:T(4,128)S(1)} %copy.17.send_member, bf16[512,768]{1,0:T(8,128)(2,1)S(1)} %get-tuple-element.34.back, bf16[512,768]{1,0:T(8,128)(2,1)S(1)} %copy-done.4, ...), custom_call_target="tpu_custom_call" | custom-call | tf_op jit(solution)/shard_map/sweep/pallas_call | solution.py:321
  93.8 7.1 %collective-permute-start.26 = (bf16[256,768]{1,0:T(8,128)(2,1)S(1)}, bf16[256,768]{1,0:T(8,128)(2,1)S(1)}, u32[]{:S(2)}, u32[]{:S(2)}) collective-permute-start(bf16[256,768]{1,0:T(8,128)(2,1)S(1)} %copy-done.14), channel_id=1, source_target_pairs={{0,6},{1,7},{6,0},{7,1},{8,14},{9,15},{14,8},{15,9},{16,22},{17,23... | collective-permute-start | bytes 1179656 | tf_op jit(solution)/shard_map/ppermute | solution.py:209
  100.9 4.3 %collective-permute-start.28 = (bf16[256,768]{1,0:T(8,128)(2,1)S(1)}, bf16[256,768]{1,0:T(8,128)(2,1)S(1)}, u32[]{:S(2)}, u32[]{:S(2)}) collective-permute-start(bf16[256,768]{1,0:T(8,128)(2,1)S(1)} %copy-done.12), channel_id=1, source_target_pairs={{0,7},{1,6},{6,1},{7,0},{8,15},{9,14},{14,9},{15,8},{16,23},{17,22... | collective-permute-start | bytes 1179656 | tf_op jit(solution)/shard_map/ppermute | solution.py:209
  115.2 6.3 %collective-permute-done.26.rest_8_ = bf16[256,768]{1,0:T(8,128)(2,1)S(1)} collective-permute-done((bf16[256,768]{1,0:T(8,128)(2,1)S(1)}, bf16[256,768]{1,0:T(8,128)(2,1)S(1)}, u32[]{:S(2)}, u32[]{:S(2)}) %collective-permute-start.26) | collective-permute-done | bytes 393248 | tf_op jit(solution)/shard_map/ppermute | solution.py:209
  121.5 6.3 %collective-permute-done.28.rest_10_ = bf16[256,768]{1,0:T(8,128)(2,1)S(1)} collective-permute-done((bf16[256,768]{1,0:T(8,128)(2,1)S(1)}, bf16[256,768]{1,0:T(8,128)(2,1)S(1)}, u32[]{:S(2)}, u32[]{:S(2)}) %collective-permute-start.28) | collective-permute-done | bytes 393248 | tf_op jit(solution)/shard_map/ppermute | solution.py:209
  127.8 8.1 %collective-permute-done.23.rest_4_ = bf16[256,768]{1,0:T(8,128)(2,1)S(1)} collective-permute-done((bf16[256,768]{1,0:T(8,128)(2,1)S(1)}, bf16[256,768]{1,0:T(8,128)(2,1)S(1)}, u32[]{:S(2)}, u32[]{:S(2)}) %collective-permute-start.23) | collective-permute-done | bytes 393248 | tf_op jit(solution)/shard_map/ppermute | solution.py:209
  138.7 10.4 %middle.1 = (f32[2,256,768]{2,1,0:T(8,128)}, bf16[512,768]{1,0:T(8,128)(2,1)}, bf16[512,768]{1,0:T(8,128)(2,1)}, bf16[256,768]{1,0:T(8,128)(2,1)S(1)}, bf16[256,...) custom-call(s32[1,8]{1,0:T(1,128)S(1)} %copy-done.9, ...), custom_call_target="tpu_custom_call" | custom-call | tf_op jit(solution)/shard_map/middle/pallas_call | solution.py:354
  156.2 5.6 %collective-permute-start.33 = (bf16[96,768]{1,0:T(8,128)(2,1)S(1)}, bf16[96,768]{1,0:T(8,128)(2,1)S(1)}, u32[]{:S(2)}, u32[]{:S(2)}) collective-permute-start(bf16[96,768]{1,0:T(8,128)(2,1)S(1)} %get-tuple-element.69), channel_id=1, source_target_pairs={{0,8},{8,16},{16,24},{24,0},{1,9},{9,17},{17,25},{25,1},{2,10},{10... | collective-permute-start | bytes 442376 | tf_op jit(solution)/shard_map/ppermute | solution.py:270
  164.0 4.2 %collective-permute-done.33 = bf16[96,768]{1,0:T(8,128)(2,1)S(1)} collective-permute-done((bf16[96,768]{1,0:T(8,128)(2,1)S(1)}, bf16[96,768]{1,0:T(8,128)(2,1)S(1)}, u32[]{:S(2)}, u32[]{:S(2)}) %collective-permute-start.33) | collective-permute-done | bytes 147488 | tf_op jit(solution)/shard_map/ppermute | solution.py:270
  193.6 15.9 %collective-permute-done.43 = bf16[96,768]{1,0:T(8,128)(2,1)S(1)} collective-permute-done((bf16[96,768]{1,0:T(8,128)(2,1)S(1)}, bf16[96,768]{1,0:T(8,128)(2,1)S(1)}, u32[]{:S(2)}, u32[]{:S(2)}) %collective-permute-start.43) | collective-permute-done | bytes 147488 | tf_op jit(solution)/shard_map/ppermute | solution.py:279
  209.5 5.7 %collective-permute-done.44 = bf16[96,768]{1,0:T(8,128)(2,1)S(1)} collective-permute-done((bf16[96,768]{1,0:T(8,128)(2,1)S(1)}, bf16[96,768]{1,0:T(8,128)(2,1)S(1)}, u32[]{:S(2)}, u32[]{:S(2)}) %collective-permute-start.44) | collective-permute-done | bytes 147488 | tf_op jit(solution)/shard_map/ppermute | solution.py:279
  222.4 4.1 %sweep.3.base = f32[2,256,768]{2,1,0:T(8,128)S(1)} custom-call(s32[1,24]{1,0:T(1,128)S(1)} %copy-done.10, s32[1,24]{1,0:T(1,128)S(1)} %copy-done.7, s32[1]{0:T(128)S(6)} %copy.38.block_count, s32[1,4,1]{2,1,0:T(4,128)S(1)} %copy.17.send_member, bf16[512,768]{1,0:T(8,128)(2,1)S(1)} %copy-done.6, f32[2,256,768]{2,1,0:T(8,128)S(1)} %copy-done.5, ...), custom_call_target="tpu_custom_call" | custom-call | tf_op jit(solution)/shard_map/sweep/pallas_call | solution.py:321
  227.9 6.5 %collective-permute-start.54 = (bf16[256,768]{1,0:T(8,128)(2,1)S(1)}, bf16[256,768]{1,0:T(8,128)(2,1)S(1)}, u32[]{:S(2)}, u32[]{:S(2)}) collective-permute-start(bf16[256,768]{1,0:T(8,128)(2,1)S(1)} %get-tuple-element.62), channel_id=1, source_target_pairs={{0,6},{1,7},{6,0},{7,1},{8,14},{9,15},{14,8},{15,9},{16,22},{17,23... | collective-permute-start | bytes 1179656 | tf_op jit(solution)/shard_map/ppermute | solution.py:209
  234.5 4.9 %collective-permute-start.56 = (bf16[256,768]{1,0:T(8,128)(2,1)S(1)}, bf16[256,768]{1,0:T(8,128)(2,1)S(1)}, u32[]{:S(2)}, u32[]{:S(2)}) collective-permute-start(bf16[256,768]{1,0:T(8,128)(2,1)S(1)} %get-tuple-element.64), channel_id=1, source_target_pairs={{0,7},{1,6},{6,1},{7,0},{8,15},{9,14},{14,9},{15,8},{16,23},{17,22... | collective-permute-start | bytes 1179656 | tf_op jit(solution)/shard_map/ppermute | solution.py:209
  244.2 7.1 %collective-permute-done.52.rest_5_ = bf16[256,768]{1,0:T(8,128)(2,1)S(1)} collective-permute-done((bf16[256,768]{1,0:T(8,128)(2,1)S(1)}, bf16[256,768]{1,0:T(8,128)(2,1)S(1)}, u32[]{:S(2)}, u32[]{:S(2)}) %collective-permute-start.52) | collective-permute-done | bytes 393248 | tf_op jit(solution)/shard_map/ppermute | solution.py:209
  255.0 7.3 %collective-permute-done.54.rest_8_ = bf16[256,768]{1,0:T(8,128)(2,1)S(1)} collective-permute-done((bf16[256,768]{1,0:T(8,128)(2,1)S(1)}, bf16[256,768]{1,0:T(8,128)(2,1)S(1)}, u32[]{:S(2)}, u32[]{:S(2)}) %collective-permute-start.54) | collective-permute-done | bytes 393248 | tf_op jit(solution)/shard_map/ppermute | solution.py:209
  262.3 7.2 %collective-permute-done.56.rest_10_ = bf16[256,768]{1,0:T(8,128)(2,1)S(1)} collective-permute-done((bf16[256,768]{1,0:T(8,128)(2,1)S(1)}, bf16[256,768]{1,0:T(8,128)(2,1)S(1)}, u32[]{:S(2)}, u32[]{:S(2)}) %collective-permute-start.56) | collective-permute-done | bytes 393248 | tf_op jit(solution)/shard_map/ppermute | solution.py:209
  269.5 4.5 %collective-permute-done.51.rest_4_ = bf16[256,768]{1,0:T(8,128)(2,1)S(1)} collective-permute-done((bf16[256,768]{1,0:T(8,128)(2,1)S(1)}, bf16[256,768]{1,0:T(8,128)(2,1)S(1)}, u32[]{:S(2)}, u32[]{:S(2)}) %collective-permute-start.51) | collective-permute-done | bytes 393248 | tf_op jit(solution)/shard_map/ppermute | solution.py:209
  274.0 4.9 %collective-permute-done.53.rest_6_ = bf16[256,768]{1,0:T(8,128)(2,1)S(1)} collective-permute-done((bf16[256,768]{1,0:T(8,128)(2,1)S(1)}, bf16[256,768]{1,0:T(8,128)(2,1)S(1)}, u32[]{:S(2)}, u32[]{:S(2)}) %collective-permute-start.53) | collective-permute-done | bytes 393248 | tf_op jit(solution)/shard_map/ppermute | solution.py:209
  278.9 6.2 %last.1 = bf16[512,768]{1,0:T(8,128)(2,1)} custom-call(s32[1,24]{1,0:T(1,128)S(1)} %copy-done.7, s32[1,8]{1,0:T(1,128)S(1)} %collective-permute-done.far_table, f32[2,256,768]{2,1,0:T(8,128)} %copy-done.1, bf16[24,256,256]{2,1,0:T(8,128)(2,1)} %values.7, f32[768,768]{1,0:T(8,128)} %bitcast.134, bf16[256,768]{1,0:T(8,128)(2,1)S(1)} %collective-permute-done.46.rest_0_, ...), custom_call_target="tpu_custom_call" | custom-call | tf_op jit(solution)/shard_map/last/pallas_call | solution.py:372
  (193 shorter events, 131.0 us)
Async XLA Ops:
  54.9 26.2 %collective-permute-start.22 = (bf16[512,768]{1,0:T(8,128)(2,1)S(1)}, bf16[512,768]{1,0:T(8,128)(2,1)S(1)}, u32[]{:S(2)}, u32[]{:S(2)}) collective-permute-start(bf16[512,768]{1,0:T(8,128)(2,1)S(1)} %get-tuple-element.34.back), channel_id=1, source_target_pairs={{2,4},{3,5},{4,2},{5,3},{10,12},{11,13},{12,10},{13,11},{18,20},{1... | collective-permute-start | bytes 2359304 | tf_op jit(solution)/shard_map/ppermute | solution.py:209
  68.5 43.4 %collective-permute-start.17 = (bf16[384,768]{1,0:T(8,128)(2,1)}, bf16[384,768]{1,0:T(8,128)(2,1)}, u32[]{:S(2)}, u32[]{:S(2)}) collective-permute-start(bf16[384,768]{1,0:T(8,128)(2,1)} %bitcast.25), channel_id=1, source_target_pairs={{0,1},{1,0},{2,3},{3,2},{4,5},{5,4},{6,7},{7,6},{8,9},{9,8},{10,11... | collective-permute-start | bytes 1769480 | tf_op jit(solution)/shard_map/ppermute | solution.py:279
  75.4 18.3 %collective-permute-start.19 = (bf16[256,768]{1,0:T(8,128)(2,1)}, bf16[256,768]{1,0:T(8,128)(2,1)S(1)}, u32[]{:S(2)}, u32[]{:S(2)}) collective-permute-start(bf16[256,768]{1,0:T(8,128)(2,1)} %copy-done.18), channel_id=1, source_target_pairs={{0,2},{1,3},{2,0},{3,1},{4,6},{5,7},{6,4},{7,5},{8,10},{9,11},{10,... | collective-permute-start | bytes 1179656 | tf_op jit(solution)/shard_map/ppermute | solution.py:209
  78.2 22.6 %collective-permute-start.20 = (bf16[256,768]{1,0:T(8,128)(2,1)}, bf16[256,768]{1,0:T(8,128)(2,1)S(1)}, u32[]{:S(2)}, u32[]{:S(2)}) collective-permute-start(bf16[256,768]{1,0:T(8,128)(2,1)} %copy-done.17), channel_id=1, source_target_pairs={{0,3},{1,2},{2,1},{3,0},{4,7},{5,6},{6,5},{7,4},{8,11},{9,10},{10,... | collective-permute-start | bytes 1179656 | tf_op jit(solution)/shard_map/ppermute | solution.py:209
  78.2 26.9 %collective-permute-start.21 = (bf16[256,768]{1,0:T(8,128)(2,1)}, bf16[256,768]{1,0:T(8,128)(2,1)S(1)}, u32[]{:S(2)}, u32[]{:S(2)}) collective-permute-start(bf16[256,768]{1,0:T(8,128)(2,1)} %copy-done.16), channel_id=1, source_target_pairs={{0,4},{1,5},{6,2},{7,3},{8,12},{9,13},{14,10},{15,11},{16,20},{17,... | collective-permute-start | bytes 1179656 | tf_op jit(solution)/shard_map/ppermute | solution.py:209
  81.2 29.3 %collective-permute-start.24 = (bf16[256,768]{1,0:T(8,128)(2,1)}, bf16[256,768]{1,0:T(8,128)(2,1)S(1)}, u32[]{:S(2)}, u32[]{:S(2)}) collective-permute-start(bf16[256,768]{1,0:T(8,128)(2,1)} %copy-done.15), channel_id=1, source_target_pairs={{0,5},{1,4},{6,3},{7,2},{8,13},{9,12},{14,11},{15,10},{16,21},{17,... | collective-permute-start | bytes 1179656 | tf_op jit(solution)/shard_map/ppermute | solution.py:209
  93.8 27.7 %collective-permute-start.26 = (bf16[256,768]{1,0:T(8,128)(2,1)S(1)}, bf16[256,768]{1,0:T(8,128)(2,1)S(1)}, u32[]{:S(2)}, u32[]{:S(2)}) collective-permute-start(bf16[256,768]{1,0:T(8,128)(2,1)S(1)} %copy-done.14), channel_id=1, source_target_pairs={{0,6},{1,7},{6,0},{7,1},{8,14},{9,15},{14,8},{15,9},{16,22},{17,23... | collective-permute-start | bytes 1179656 | tf_op jit(solution)/shard_map/ppermute | solution.py:209
  100.9 27.0 %collective-permute-start.28 = (bf16[256,768]{1,0:T(8,128)(2,1)S(1)}, bf16[256,768]{1,0:T(8,128)(2,1)S(1)}, u32[]{:S(2)}, u32[]{:S(2)}) collective-permute-start(bf16[256,768]{1,0:T(8,128)(2,1)S(1)} %copy-done.12), channel_id=1, source_target_pairs={{0,7},{1,6},{6,1},{7,0},{8,15},{9,14},{14,9},{15,8},{16,23},{17,22... | collective-permute-start | bytes 1179656 | tf_op jit(solution)/shard_map/ppermute | solution.py:209
  105.2 30.7 %collective-permute-start.23 = (bf16[256,768]{1,0:T(8,128)(2,1)S(1)}, bf16[256,768]{1,0:T(8,128)(2,1)S(1)}, u32[]{:S(2)}, u32[]{:S(2)}) collective-permute-start(bf16[256,768]{1,0:T(8,128)(2,1)S(1)} %get-tuple-element.43), channel_id=1, source_target_pairs={{2,0},{3,1},{4,6},{5,7},{10,8},{11,9},{12,14},{13,15},{18,16},{19,... | collective-permute-start | bytes 1179656 | tf_op jit(solution)/shard_map/ppermute | solution.py:209
  110.5 27.3 %collective-permute-start.25 = (bf16[256,768]{1,0:T(8,128)(2,1)S(1)}, bf16[256,768]{1,0:T(8,128)(2,1)S(1)}, u32[]{:S(2)}, u32[]{:S(2)}) collective-permute-start(bf16[256,768]{1,0:T(8,128)(2,1)S(1)} %get-tuple-element.45), channel_id=1, source_target_pairs={{2,1},{3,0},{4,7},{5,6},{10,9},{11,8},{12,15},{13,14},{18,17},{19,... | collective-permute-start | bytes 1179656 | tf_op jit(solution)/shard_map/ppermute | solution.py:209
  111.8 26.0 %collective-permute-start.27 = (bf16[256,768]{1,0:T(8,128)(2,1)S(1)}, bf16[256,768]{1,0:T(8,128)(2,1)S(1)}, u32[]{:S(2)}, u32[]{:S(2)}) collective-permute-start(bf16[256,768]{1,0:T(8,128)(2,1)S(1)} %get-tuple-element.47), channel_id=1, source_target_pairs={{2,3},{3,2},{4,5},{5,4},{10,11},{11,10},{12,13},{13,12},{18,19},{1... | collective-permute-start | bytes 1179656 | tf_op jit(solution)/shard_map/ppermute | solution.py:209
  187.0 28.3 %collective-permute-start.29 = (bf16[256,768]{1,0:T(8,128)(2,1)S(1)}, bf16[256,768]{1,0:T(8,128)(2,1)S(1)}, u32[]{:S(2)}, u32[]{:S(2)}) collective-permute-start(bf16[256,768]{1,0:T(8,128)(2,1)S(1)} %get-tuple-element.51), channel_id=1, source_target_pairs={{0,8},{8,16},{16,24},{24,0},{1,9},{9,17},{17,25},{25,1},{2,10},{10... | collective-permute-start | bytes 1179656 | tf_op jit(solution)/shard_map/ppermute | solution.py:243
  187.4 28.5 %collective-permute-start.30 = (bf16[256,768]{1,0:T(8,128)(2,1)S(1)}, bf16[256,768]{1,0:T(8,128)(2,1)S(1)}, u32[]{:S(2)}, u32[]{:S(2)}) collective-permute-start(bf16[256,768]{1,0:T(8,128)(2,1)S(1)} %get-tuple-element.52), channel_id=1, source_target_pairs={{0,16},{8,24},{16,0},{24,8},{1,17},{9,25},{17,1},{25,9},{2,18},{10... | collective-permute-start | bytes 1179656 | tf_op jit(solution)/shard_map/ppermute | solution.py:243
  188.8 27.8 %collective-permute-start.31 = (bf16[256,768]{1,0:T(8,128)(2,1)S(1)}, bf16[256,768]{1,0:T(8,128)(2,1)S(1)}, u32[]{:S(2)}, u32[]{:S(2)}) collective-permute-start(bf16[256,768]{1,0:T(8,128)(2,1)S(1)} %get-tuple-element.53), channel_id=1, source_target_pairs={{0,24},{8,0},{16,8},{24,16},{1,25},{9,1},{17,9},{25,17},{2,26},{10... | collective-permute-start | bytes 1179656 | tf_op jit(solution)/shard_map/ppermute | solution.py:243
  190.7 30.4 %collective-permute-start.50 = (bf16[512,768]{1,0:T(8,128)(2,1)S(1)}, bf16[512,768]{1,0:T(8,128)(2,1)S(1)}, u32[]{:S(2)}, u32[]{:S(2)}) collective-permute-start(bf16[512,768]{1,0:T(8,128)(2,1)S(1)} %copy-done.6), channel_id=1, source_target_pairs={{2,4},{3,5},{4,2},{5,3},{10,12},{11,13},{12,10},{13,11},{18,20},{1... | collective-permute-start | bytes 2359304 | tf_op jit(solution)/shard_map/ppermute | solution.py:209
  215.3 37.3 %collective-permute-start.45 = (bf16[384,768]{1,0:T(8,128)(2,1)S(1)}, bf16[384,768]{1,0:T(8,128)(2,1)S(1)}, u32[]{:S(2)}, u32[]{:S(2)}) collective-permute-start(bf16[384,768]{1,0:T(8,128)(2,1)S(1)} %bitcast.140), channel_id=1, source_target_pairs={{0,1},{1,0},{2,3},{3,2},{4,5},{5,4},{6,7},{7,6},{8,9},{9,8},{10,11... | collective-permute-start | bytes 1769480 | tf_op jit(solution)/shard_map/ppermute | solution.py:279
  216.6 18.0 %collective-permute-start.48 = (bf16[256,768]{1,0:T(8,128)(2,1)S(1)}, bf16[256,768]{1,0:T(8,128)(2,1)S(1)}, u32[]{:S(2)}, u32[]{:S(2)}) collective-permute-start(bf16[256,768]{1,0:T(8,128)(2,1)S(1)} %get-tuple-element.57), channel_id=1, source_target_pairs={{0,3},{1,2},{2,1},{3,0},{4,7},{5,6},{6,5},{7,4},{8,11},{9,10},{10,... | collective-permute-start | bytes 1179656 | tf_op jit(solution)/shard_map/ppermute | solution.py:209
  217.3 25.6 %collective-permute-start.49 = (bf16[256,768]{1,0:T(8,128)(2,1)S(1)}, bf16[256,768]{1,0:T(8,128)(2,1)S(1)}, u32[]{:S(2)}, u32[]{:S(2)}) collective-permute-start(bf16[256,768]{1,0:T(8,128)(2,1)S(1)} %get-tuple-element.58), channel_id=1, source_target_pairs={{0,4},{1,5},{6,2},{7,3},{8,12},{9,13},{14,10},{15,11},{16,20},{17,... | collective-permute-start | bytes 1179656 | tf_op jit(solution)/shard_map/ppermute | solution.py:209
  221.1 30.3 %collective-permute-start.52 = (bf16[256,768]{1,0:T(8,128)(2,1)S(1)}, bf16[256,768]{1,0:T(8,128)(2,1)S(1)}, u32[]{:S(2)}, u32[]{:S(2)}) collective-permute-start(bf16[256,768]{1,0:T(8,128)(2,1)S(1)} %get-tuple-element.60), channel_id=1, source_target_pairs={{0,5},{1,4},{6,3},{7,2},{8,13},{9,12},{14,11},{15,10},{16,21},{17,... | collective-permute-start | bytes 1179656 | tf_op jit(solution)/shard_map/ppermute | solution.py:209
  227.9 34.4 %collective-permute-start.54 = (bf16[256,768]{1,0:T(8,128)(2,1)S(1)}, bf16[256,768]{1,0:T(8,128)(2,1)S(1)}, u32[]{:S(2)}, u32[]{:S(2)}) collective-permute-start(bf16[256,768]{1,0:T(8,128)(2,1)S(1)} %get-tuple-element.62), channel_id=1, source_target_pairs={{0,6},{1,7},{6,0},{7,1},{8,14},{9,15},{14,8},{15,9},{16,22},{17,23... | collective-permute-start | bytes 1179656 | tf_op jit(solution)/shard_map/ppermute | solution.py:209
  234.5 35.0 %collective-permute-start.56 = (bf16[256,768]{1,0:T(8,128)(2,1)S(1)}, bf16[256,768]{1,0:T(8,128)(2,1)S(1)}, u32[]{:S(2)}, u32[]{:S(2)}) collective-permute-start(bf16[256,768]{1,0:T(8,128)(2,1)S(1)} %get-tuple-element.64), channel_id=1, source_target_pairs={{0,7},{1,6},{6,1},{7,0},{8,15},{9,14},{14,9},{15,8},{16,23},{17,22... | collective-permute-start | bytes 1179656 | tf_op jit(solution)/shard_map/ppermute | solution.py:209
  242.9 31.1 %collective-permute-start.51 = (bf16[256,768]{1,0:T(8,128)(2,1)S(1)}, bf16[256,768]{1,0:T(8,128)(2,1)S(1)}, u32[]{:S(2)}, u32[]{:S(2)}) collective-permute-start(bf16[256,768]{1,0:T(8,128)(2,1)S(1)} %get-tuple-element.59), channel_id=1, source_target_pairs={{2,0},{3,1},{4,6},{5,7},{10,8},{11,9},{12,14},{13,15},{18,16},{19,... | collective-permute-start | bytes 1179656 | tf_op jit(solution)/shard_map/ppermute | solution.py:209
  251.4 27.5 %collective-permute-start.53 = (bf16[256,768]{1,0:T(8,128)(2,1)S(1)}, bf16[256,768]{1,0:T(8,128)(2,1)S(1)}, u32[]{:S(2)}, u32[]{:S(2)}) collective-permute-start(bf16[256,768]{1,0:T(8,128)(2,1)S(1)} %get-tuple-element.61), channel_id=1, source_target_pairs={{2,1},{3,0},{4,7},{5,6},{10,9},{11,8},{12,15},{13,14},{18,17},{19,... | collective-permute-start | bytes 1179656 | tf_op jit(solution)/shard_map/ppermute | solution.py:209
  252.7 26.2 %collective-permute-start.55 = (bf16[256,768]{1,0:T(8,128)(2,1)S(1)}, bf16[256,768]{1,0:T(8,128)(2,1)S(1)}, u32[]{:S(2)}, u32[]{:S(2)}) collective-permute-start(bf16[256,768]{1,0:T(8,128)(2,1)S(1)} %get-tuple-element.63), channel_id=1, source_target_pairs={{2,3},{3,2},{4,5},{5,4},{10,11},{11,10},{12,13},{13,12},{18,19},{1... | collective-permute-start | bytes 1179656 | tf_op jit(solution)/shard_map/ppermute | solution.py:209
  (60 other events, 544.4 us)
where the time goes:
time: 288 us; the launch traced here: 285 us
  waiting for transfers between devices  129 us (45%)
  starting transfers between devices  88 us (31%)
  Pallas kernels  33 us (11%)
  local copies, waits for them, and re-layouts  20.3 us (7%)
  matrix products  7.64 us (3%)
  other arithmetic  5.45 us (2%)
    ppermute x22, waiting for transfers between devices, permute(): lax.ppermute(block, 'group', [(g, g ^ peer) for g in range(groups) if kee...  61.4 us
    ppermute x22, starting transfers between devices, permute(): lax.ppermute(block, 'group', [(g, g ^ peer) for g in range(groups) if kee...  42.5 us
    ppermute x14, waiting for transfers between devices, weight_total(): block = lax.ppermute(part, axis, perm)  33.6 us
    ppermute x14, waiting for transfers between devices, weight_total(): lax.ppermute(piece(shift).astype(BF16), axis, perm)  25.1 us
    ppermute x14, starting transfers between devices, weight_total(): lax.ppermute(piece(shift).astype(BF16), axis, perm)  22.5 us
    ppermute x14, starting transfers between devices, weight_total(): block = lax.ppermute(part, axis, perm)  15.2 us
    pallas_call x1, Pallas kernels, body(): pl.pallas_call(functools.partial(middle_kernel, rows, plan), out_shape=[t...  10.4 us
    ppermute x6, waiting for transfers between devices, member_exchange(): lax.ppermute(block, 'member', [(m, (m + 1 + place // capacity) % members)...  8.64 us
  transfers between devices with their start and end apart: 57, of which 34 were waited for; matrix products, arithmetic and copies ran while one was open for 5% of the time, Pallas kernels for 4%

commit v1 on v0

--- a/solution.py
+++ b/solution.py
@@ -13,7 +13,7 @@
 VMEM = pl.BlockSpec(memory_space=pltpu.VMEM)
 SMEM = pl.BlockSpec(memory_space=pltpu.SMEM)
 ANY = pl.BlockSpec(memory_space=pl.ANY)
-LIMIT = 48 << 20
+LIMIT = 20 << 20
 PAIR = 2
 
 
@@ -247,43 +247,91 @@
 
 def stage_peers(axis, stride, size):
     total = lax.axis_size(axis)
-
-    def moved(index, shift):
-        place = index // stride % size
-        return index + ((place + shift) % size - place) * stride
-
-    perms = [[(i, moved(i, shift)) for i in range(total)] for shift in range(1, size)]
+    perms = [[(i, i ^ (s * stride)) for i in range(total)] for s in range(1, size)]
     return lax.axis_index(axis) // stride % size, perms
 
 
-def weight_total(part):
+def kernel_call(kernel, out_shape, operands, scratch=(), outs_any=False):
+    return pl.pallas_call(
+        kernel,
+        out_shape=out_shape,
+        in_specs=[VMEM] * len(operands),
+        out_specs=jax.tree.map(lambda _: ANY if outs_any else VMEM, out_shape),
+        scratch_shapes=list(scratch),
+        compiler_params=params(),
+    )(*operands)
+
+
+def part_kernel(agg, pull, keep, give):
+    place = lax.rem(lax.axis_index("group"), PAIR)
+    half = keep.shape[0]
+    for number in range(PAIR):
+        part = turned_dot(agg[:, number * half : (number + 1) * half], pull[...])
+
+        @pl.when(place == number)
+        def _():
+            keep[...] = part
+
+        @pl.when(place != number)
+        def _():
+            give[...] = part.astype(BF16)
+
+
+def split_kernel(keep, got, own, *gives):
+    place = lax.axis_index("member")
+    size = own.shape[0]
+    for number, out in enumerate((own,) + gives):
+        part = pl.ds(pl.multiple_of((place ^ number) * size, size), size)
+        out[...] = (keep[part, :] + got[part, :].astype(F32)).astype(out.dtype)
+
+
+def join_kernel(*refs):
+    *pieces, out = refs
+    place = lax.axis_index("member")
+    size = pieces[0].shape[0]
+    for number, piece in enumerate(pieces):
+        out[pl.ds(pl.multiple_of((place ^ number) * size, size), size), :] = piece[...]
+
+
+def finish_kernel(scale, *refs):
+    *pieces, out = refs
+    place = lax.rem(lax.axis_index("group"), PAIR)
+    size = pieces[0].shape[0]
+    for number, piece in enumerate(pieces):
+        out[pl.ds(pl.multiple_of((place ^ number) * size, size), size), :] = piece[...].astype(F32) * scale
+
+
+def pairwise(parts):
+    while len(parts) > 1:
+        parts = [left + right for left, right in zip(parts[0::2], parts[1::2])]
+    return parts[0]
+
+
+def weight_total(aggregate, pulled, scale):
     groups, members = lax.axis_size("group"), lax.axis_size("member")
-    stages = [("group", 1, PAIR), ("member", 1, members), ("group", PAIR, groups // PAIR)]
-    for axis, stride, size in stages:
-        place, perms = stage_peers(axis, stride, size)
-        pieces = part.reshape(size, part.shape[0] // size, part.shape[1])
-
-        def piece(shift):
-            return lax.dynamic_index_in_dim(pieces, (place + shift) % size, 0, keepdims=False)
-
-        got = [
-            lax.ppermute(piece(shift).astype(BF16), axis, perm) for shift, perm in enumerate(perms, 1)
-        ]
-        part = sum((block.astype(F32) for block in got), piece(0))
-    part = part.astype(BF16)
-    for axis, stride, size in reversed(stages):
-        place, perms = stage_peers(axis, stride, size)
-        whole = jnp.zeros((size,) + part.shape, BF16)
-        whole = lax.dynamic_update_index_in_dim(whole, part, place, 0)
-        for shift, perm in enumerate(perms, 1):
-            block = lax.ppermute(part, axis, perm)
-            whole = lax.dynamic_update_index_in_dim(whole, block, (place - shift) % size, 0)
-        part = whole.reshape(size * part.shape[0], part.shape[1])
-    return part.astype(F32)
-
-
-def weight_part(aggregate, pulled):
-    return lax.dot_general(aggregate, pulled, (((0,), (0,)), ((), ())), preferred_element_type=F32)
+    width, depth = aggregate.shape[1], pulled.shape[1]
+    half, piece = width // PAIR, width // PAIR // members
+    _, pair_perms = stage_peers("group", 1, PAIR)
+    _, member_perms = stage_peers("member", 1, members)
+    _, line_perms = stage_peers("group", PAIR, groups // PAIR)
+
+    def permute(blocks, axis, perms):
+        return [lax.ppermute(block, axis, perm) for block, perm in zip(blocks, perms)]
+
+    def shape(rows, dtype):
+        return jax.ShapeDtypeStruct((rows, depth), dtype)
+
+    keep, give = kernel_call(part_kernel, [shape(half, F32), shape(half, BF16)], (aggregate, pulled))
+    (got,) = permute([give], "group", pair_perms)
+    own, *gives = kernel_call(split_kernel, [shape(piece, F32)] + [shape(piece, BF16)] * (members - 1), (keep, got))
+    got = permute(gives, "member", member_perms)
+    total = sum((block.astype(F32) for block in got), own).astype(BF16)
+    got = permute([total] * (groups // PAIR - 1), "group", line_perms)
+    total = pairwise([block.astype(F32) for block in [total] + got]).astype(BF16)
+    got = permute([total] * (members - 1), "member", member_perms)
+    total = kernel_call(join_kernel, shape(half, BF16), [total] + got)
+    got = permute([total], "group", pair_perms)
+    return kernel_call(functools.partial(finish_kernel, scale), shape(width, F32), [total] + got)
 
 
 def body(
@@ -331,11 +379,11 @@
             name="sweep",
         )(src_slot, dst_block, block_count, send_member, back, base, block_values, *received)
 
+    plan = [1, 1, 1, 2, 2, 2, 2] if relayed(groups) else [1] * cross
+
     far_table = send_group
     if relayed(groups):
         far_table = lax.ppermute(send_group, "group", [(g, g ^ 6) for g in range(groups)])
-    plan = [1, 1, 1, 2, 2, 2, 2] if relayed(groups) else [1] * cross
-
     pull_two, back_two, *outs = pl.pallas_call(
         functools.partial(first_kernel, rows, cross),
         out_shape=[field, field] + sends,
@@ -348,7 +396,7 @@
     from_group = group_exchange(rows, back_two, outs[:cross], far_table)
     from_member = member_exchange(outs[cross:], capacity)
     slope_one = silu_slope(jnp.dot(agg_one, hop_one_weight, preferred_element_type=F32))
-    grad_w_two = weight_total(weight_part(agg_two, pull_two)) * grad_scale
+    grad_w_two = weight_total(agg_two, pull_two, grad_scale)
     base_two = sweep(back_two, grad_out, from_member)
 
     carry, pull_one, back_one, *outs = pl.pallas_call(
@@ -366,7 +414,7 @@
     )
     from_group = group_exchange(rows, back_one, outs[:cross], far_table)
     from_member = member_exchange(outs[cross:], capacity)
-    grad_w_one = weight_total(weight_part(agg_one, pull_one)) * grad_scale
+    grad_w_one = weight_total(agg_one, pull_one, grad_scale)
     base_one = sweep(back_one, carry, from_member)
 
     grad_emb = pl.pallas_call(

time: 288 us -> 272 us (0.944)
  the two profiles are of different devices: /device:TPU:4 before, /device:TPU:3 now
where the time goes in v1:
time: 272 us; the launch traced here: 271 us
  waiting for transfers between devices  136 us (50%)
  starting transfers between devices  85.2 us (31%)
  Pallas kernels  37.8 us (14%)
  local copies, waits for them, and re-layouts  9.2 us (3%)
    ppermute x22, waiting for transfers between devices, permute(): lax.ppermute(block, 'group', [(g, g ^ peer) for g in range(groups) if kee...  68.2 us
    ppermute x22, starting transfers between devices, permute(): lax.ppermute(block, 'group', [(g, g ^ peer) for g in range(groups) if kee...  61.5 us
    ppermute x22, waiting for transfers between devices, permute(): lax.ppermute(block, axis, perm)  44.2 us
    ppermute x6, waiting for transfers between devices, member_exchange(): lax.ppermute(block, 'member', [(m, (m + 1 + place // capacity) % members)...  20.4 us
    ppermute x22, starting transfers between devices, permute(): lax.ppermute(block, axis, perm)  19.1 us
    pallas_call x2, Pallas kernels, sweep(): pl.pallas_call(functools.partial(sweep_kernel, rows, cross), out_shape=to...  9.89 us
    unnamed x29, local copies, waits for them, and re-layouts  9.2 us
    pallas_call x1, Pallas kernels, body(): pl.pallas_call(functools.partial(middle_kernel, rows, plan), out_shape=[t...  8.77 us
  transfers between devices with their start and end apart: 51, of which 28 were waited for; matrix products, arithmetic and copies ran while one was open for 0% of the time, Pallas kernels for 6%

profile of v1, /device:TPU:3, one launch (start us, length us, event | category | flops | bytes accessed | tf_op | source)
XLA Modules:
  0.0 271.1 jit_solution(4247120626059116503)
XLA Ops:
  5.6 4.2 %first.1 = (bf16[512,768]{1,0:T(8,128)(2,1)S(1)}, bf16[512,768]{1,0:T(8,128)(2,1)S(1)}, bf16[256,768]{1,0:T(8,128)(2,1)S(1)}, bf16[256,768]{1,0:T(8,128)(2,1)S(1...) custom-call(s32[1,8]{1,0:T(1,128)S(1)} %copy-done.11, ...), custom_call_target="tpu_custom_call" | custom-call | tf_op jit(solution)/shard_map/first/pallas_call | solution.py:387
  18.8 4.0 %collective-permute-done.7 = bf16[96,768]{1,0:T(8,128)(2,1)S(1)} collective-permute-done((bf16[96,768]{1,0:T(8,128)(2,1)S(1)}, bf16[96,768]{1,0:T(8,128)(2,1)S(1)}, u32[]{:S(2)}, u32[]{:S(2)}) %collective-permute-start.7) | collective-permute-done | bytes 147488 | tf_op jit(solution)/shard_map/ppermute | solution.py:319
  28.9 9.5 %collective-permute-done.9 = bf16[96,768]{1,0:T(8,128)(2,1)S(1)} collective-permute-done((bf16[96,768]{1,0:T(8,128)(2,1)S(1)}, bf16[96,768]{1,0:T(8,128)(2,1)S(1)}, u32[]{:S(2)}, u32[]{:S(2)}) %collective-permute-start.9) | collective-permute-done | bytes 147488 | tf_op jit(solution)/shard_map/ppermute | solution.py:319
  48.6 6.4 %collective-permute-start.15 = (bf16[256,768]{1,0:T(8,128)(2,1)S(1)}, bf16[256,768]{1,0:T(8,128)(2,1)S(1)}, u32[]{:S(2)}, u32[]{:S(2)}) collective-permute-start(bf16[256,768]{1,0:T(8,128)(2,1)S(1)} %get-tuple-element.57), channel_id=1, source_target_pairs={{0,1},{1,0},{2,3},{3,2},{4,5},{5,4},{6,7},{7,6},{8,9},{9,8},{10,11... | collective-permute-start | bytes 1179656 | tf_op jit(solution)/shard_map/ppermute | solution.py:209
  55.2 7.5 %collective-permute-done.2.rest_1_ = bf16[256,768]{1,0:T(8,128)(2,1)S(1)} collective-permute-done((bf16[256,768]{1,0:T(8,128)(2,1)S(1)}, bf16[256,768]{1,0:T(8,128)(2,1)S(1)}, u32[]{:S(2)}, u32[]{:S(2)}) %collective-permute-start.2) | collective-permute-done | bytes 393248 | tf_op jit(solution)/shard_map/ppermute | solution.py:243
  62.6 10.8 %collective-permute-start.16 = (bf16[256,768]{1,0:T(8,128)(2,1)S(1)}, bf16[256,768]{1,0:T(8,128)(2,1)S(1)}, u32[]{:S(2)}, u32[]{:S(2)}) collective-permute-start(bf16[256,768]{1,0:T(8,128)(2,1)S(1)} %get-tuple-element.58), channel_id=1, source_target_pairs={{0,2},{1,3},{2,0},{3,1},{4,6},{5,7},{6,4},{7,5},{8,10},{9,11},{10,... | collective-permute-start | bytes 1179656 | tf_op jit(solution)/shard_map/ppermute | solution.py:209
  86.6 4.6 %collective-permute-done.17.rest_2_ = bf16[256,768]{1,0:T(8,128)(2,1)S(1)} collective-permute-done((bf16[256,768]{1,0:T(8,128)(2,1)S(1)}, bf16[256,768]{1,0:T(8,128)(2,1)S(1)}, u32[]{:S(2)}, u32[]{:S(2)}) %collective-permute-start.17) | collective-permute-done | bytes 393248 | tf_op jit(solution)/shard_map/ppermute | solution.py:209
  91.2 6.0 %collective-permute-start.25 = (bf16[256,768]{1,0:T(8,128)(2,1)S(1)}, bf16[256,768]{1,0:T(8,128)(2,1)S(1)}, u32[]{:S(2)}, u32[]{:S(2)}) collective-permute-start(bf16[256,768]{1,0:T(8,128)(2,1)S(1)} %get-tuple-element.66), channel_id=1, source_target_pairs={{0,7},{1,6},{6,1},{7,0},{8,15},{9,14},{14,9},{15,8},{16,23},{17,22... | collective-permute-start | bytes 1179656 | tf_op jit(solution)/shard_map/ppermute | solution.py:209
  98.5 6.2 %collective-permute-done.21.rest_5_ = bf16[256,768]{1,0:T(8,128)(2,1)S(1)} collective-permute-done((bf16[256,768]{1,0:T(8,128)(2,1)S(1)}, bf16[256,768]{1,0:T(8,128)(2,1)S(1)}, u32[]{:S(2)}, u32[]{:S(2)}) %collective-permute-start.21) | collective-permute-done | bytes 393248 | tf_op jit(solution)/shard_map/ppermute | solution.py:209
  108.8 4.9 %sweep.2.base = f32[2,256,768]{2,1,0:T(8,128)S(1)} custom-call(s32[1,24]{1,0:T(1,128)S(1)} %copy-done.13, s32[1,24]{1,0:T(1,128)S(1)} %copy-done.10, s32[1]{0:T(128)S(6)} %copy.18.block_count, s32[1,4,1]{2,1,0:T(4,128)S(1)} %copy.17.send_member, bf16[512,768]{1,0:T(8,128)(2,1)S(1)} %get-tuple-element.46.back, bf16[512,768]{1,0:T(8,128)(2,1)S(1)} %copy-done.4, ...), custom_call_target="tpu_custom_call" | custom-call | tf_op jit(solution)/shard_map/sweep/pallas_call | solution.py:369
  115.3 10.9 %collective-permute-done.25.rest_10_ = bf16[256,768]{1,0:T(8,128)(2,1)S(1)} collective-permute-done((bf16[256,768]{1,0:T(8,128)(2,1)S(1)}, bf16[256,768]{1,0:T(8,128)(2,1)S(1)}, u32[]{:S(2)}, u32[]{:S(2)}) %collective-permute-start.25) | collective-permute-done | bytes 393248 | tf_op jit(solution)/shard_map/ppermute | solution.py:209
  126.2 10.0 %collective-permute-done.22.rest_6_ = bf16[256,768]{1,0:T(8,128)(2,1)S(1)} collective-permute-done((bf16[256,768]{1,0:T(8,128)(2,1)S(1)}, bf16[256,768]{1,0:T(8,128)(2,1)S(1)}, u32[]{:S(2)}, u32[]{:S(2)}) %collective-permute-start.22) | collective-permute-done | bytes 393248 | tf_op jit(solution)/shard_map/ppermute | solution.py:209
  137.9 8.8 %middle.1 = (f32[2,256,768]{2,1,0:T(8,128)S(1)}, bf16[512,768]{1,0:T(8,128)(2,1)S(1)}, bf16[512,768]{1,0:T(8,128)(2,1)S(1)}, bf16[256,768]{1,0:T(8,128)(2,1)S(1)...) custom-call(s32[1,8]{1,0:T(1,128)S(1)} %copy-done.12, ...), custom_call_target="tpu_custom_call" | custom-call | tf_op jit(solution)/shard_map/middle/pallas_call | solution.py:402
  155.6 4.1 %collective-permute-done.32 = bf16[96,768]{1,0:T(8,128)(2,1)S(1)} collective-permute-done((bf16[96,768]{1,0:T(8,128)(2,1)S(1)}, bf16[96,768]{1,0:T(8,128)(2,1)S(1)}, u32[]{:S(2)}, u32[]{:S(2)}) %collective-permute-start.32) | collective-permute-done | bytes 147488 | tf_op jit(solution)/shard_map/ppermute | solution.py:319
  166.2 7.8 %collective-permute-done.34 = bf16[96,768]{1,0:T(8,128)(2,1)S(1)} collective-permute-done((bf16[96,768]{1,0:T(8,128)(2,1)S(1)}, bf16[96,768]{1,0:T(8,128)(2,1)S(1)}, u32[]{:S(2)}, u32[]{:S(2)}) %collective-permute-start.34) | collective-permute-done | bytes 147488 | tf_op jit(solution)/shard_map/ppermute | solution.py:319
  179.3 4.1 %collective-permute-done.37.refs_2_ = bf16[96,768]{1,0:T(8,128)(2,1)S(1)} collective-permute-done((bf16[96,768]{1,0:T(8,128)(2,1)S(1)}, bf16[96,768]{1,0:T(8,128)(2,1)S(1)}, u32[]{:S(2)}, u32[]{:S(2)}) %collective-permute-start.37) | collective-permute-done | bytes 147488 | tf_op jit(solution)/shard_map/ppermute | solution.py:319
  186.0 13.0 %collective-permute-done.27.rest_1_ = bf16[256,768]{1,0:T(8,128)(2,1)S(1)} collective-permute-done((bf16[256,768]{1,0:T(8,128)(2,1)S(1)}, bf16[256,768]{1,0:T(8,128)(2,1)S(1)}, u32[]{:S(2)}, u32[]{:S(2)}) %collective-permute-start.27) | collective-permute-done | bytes 393248 | tf_op jit(solution)/shard_map/ppermute | solution.py:243
  211.4 6.8 %collective-permute-done.42.rest_2_ = bf16[256,768]{1,0:T(8,128)(2,1)S(1)} collective-permute-done((bf16[256,768]{1,0:T(8,128)(2,1)S(1)}, bf16[256,768]{1,0:T(8,128)(2,1)S(1)}, u32[]{:S(2)}, u32[]{:S(2)}) %collective-permute-start.42) | collective-permute-done | bytes 393248 | tf_op jit(solution)/shard_map/ppermute | solution.py:209
  218.2 5.1 %collective-permute-start.50 = (bf16[256,768]{1,0:T(8,128)(2,1)S(1)}, bf16[256,768]{1,0:T(8,128)(2,1)S(1)}, u32[]{:S(2)}, u32[]{:S(2)}) collective-permute-start(bf16[256,768]{1,0:T(8,128)(2,1)S(1)} %get-tuple-element.88), channel_id=1, source_target_pairs={{0,7},{1,6},{6,1},{7,0},{8,15},{9,14},{14,9},{15,8},{16,23},{17,22... | collective-permute-start | bytes 1179656 | tf_op jit(solution)/shard_map/ppermute | solution.py:209
  224.6 6.0 %collective-permute-done.46.rest_5_ = bf16[256,768]{1,0:T(8,128)(2,1)S(1)} collective-permute-done((bf16[256,768]{1,0:T(8,128)(2,1)S(1)}, bf16[256,768]{1,0:T(8,128)(2,1)S(1)}, u32[]{:S(2)}, u32[]{:S(2)}) %collective-permute-start.46) | collective-permute-done | bytes 393248 | tf_op jit(solution)/shard_map/ppermute | solution.py:209
  232.6 4.9 %sweep.3.base = f32[2,256,768]{2,1,0:T(8,128)S(1)} custom-call(s32[1,24]{1,0:T(1,128)S(1)} %copy-done.13, s32[1,24]{1,0:T(1,128)S(1)} %copy-done.10, s32[1]{0:T(128)S(6)} %copy.18.block_count, s32[1,4,1]{2,1,0:T(4,128)S(1)} %copy.17.send_member, bf16[512,768]{1,0:T(8,128)(2,1)S(1)} %get-tuple-element.67.back, f32[2,256,768]{2,1,0:T(8,128)S(1)} %get-tuple-element.68.base, ...), custom_call_target="tpu_custom_call" | custom-call | tf_op jit(solution)/shard_map/sweep/pallas_call | solution.py:369
  242.0 10.8 %collective-permute-done.50.rest_10_ = bf16[256,768]{1,0:T(8,128)(2,1)S(1)} collective-permute-done((bf16[256,768]{1,0:T(8,128)(2,1)S(1)}, bf16[256,768]{1,0:T(8,128)(2,1)S(1)}, u32[]{:S(2)}, u32[]{:S(2)}) %collective-permute-start.50) | collective-permute-done | bytes 393248 | tf_op jit(solution)/shard_map/ppermute | solution.py:209
  252.8 10.0 %collective-permute-done.47.rest_6_ = bf16[256,768]{1,0:T(8,128)(2,1)S(1)} collective-permute-done((bf16[256,768]{1,0:T(8,128)(2,1)S(1)}, bf16[256,768]{1,0:T(8,128)(2,1)S(1)}, u32[]{:S(2)}, u32[]{:S(2)}) %collective-permute-start.47) | collective-permute-done | bytes 393248 | tf_op jit(solution)/shard_map/ppermute | solution.py:209
  264.4 6.5 %last.1 = bf16[512,768]{1,0:T(8,128)(2,1)} custom-call(s32[1,24]{1,0:T(1,128)S(1)} %copy-done.10, s32[1,8]{1,0:T(1,128)S(1)} %collective-permute-done.far_table, f32[2,256,768]{2,1,0:T(8,128)S(1)} %sweep.3.base, bf16[24,256,256]{2,1,0:T(8,128)(2,1)S(1)} %copy-done, f32[768,768]{1,0:T(8,128)S(1)} %copy-done.2, ...), custom_call_target="tpu_custom_call" | custom-call | tf_op jit(solution)/shard_map/last/pallas_call | solution.py:420
  (127 shorter events, 96.4 us)
Async XLA Ops:
  26.6 52.9 %collective-permute-start.19 = (bf16[512,768]{1,0:T(8,128)(2,1)S(1)}, bf16[512,768]{1,0:T(8,128)(2,1)S(1)}, u32[]{:S(2)}, u32[]{:S(2)}) collective-permute-start(bf16[512,768]{1,0:T(8,128)(2,1)S(1)} %get-tuple-element.46.back), channel_id=1, source_target_pairs={{2,4},{3,5},{4,2},{5,3},{10,12},{11,13},{12,10},{13,11},{18,20},{1... | collective-permute-start | bytes 2359304 | tf_op jit(solution)/shard_map/ppermute | solution.py:209
  27.4 27.7 %collective-permute-start.1 = (bf16[256,768]{1,0:T(8,128)(2,1)S(1)}, bf16[256,768]{1,0:T(8,128)(2,1)S(1)}, u32[]{:S(2)}, u32[]{:S(2)}) collective-permute-start(bf16[256,768]{1,0:T(8,128)(2,1)S(1)} %get-tuple-element.47), channel_id=1, source_target_pairs={{0,8},{8,16},{16,24},{24,0},{1,9},{9,17},{17,25},{25,1},{2,10},{10... | collective-permute-start | bytes 1179656 | tf_op jit(solution)/shard_map/ppermute | solution.py:243
  47.2 26.2 %collective-permute-start.3 = (bf16[256,768]{1,0:T(8,128)(2,1)S(1)}, bf16[256,768]{1,0:T(8,128)(2,1)S(1)}, u32[]{:S(2)}, u32[]{:S(2)}) collective-permute-start(bf16[256,768]{1,0:T(8,128)(2,1)S(1)} %get-tuple-element.49), channel_id=1, source_target_pairs={{0,24},{8,0},{16,8},{24,16},{1,25},{9,1},{17,9},{25,17},{2,26},{10... | collective-permute-start | bytes 1179656 | tf_op jit(solution)/shard_map/ppermute | solution.py:243
  48.6 27.2 %collective-permute-start.15 = (bf16[256,768]{1,0:T(8,128)(2,1)S(1)}, bf16[256,768]{1,0:T(8,128)(2,1)S(1)}, u32[]{:S(2)}, u32[]{:S(2)}) collective-permute-start(bf16[256,768]{1,0:T(8,128)(2,1)S(1)} %get-tuple-element.57), channel_id=1, source_target_pairs={{0,1},{1,0},{2,3},{3,2},{4,5},{5,4},{6,7},{7,6},{8,9},{9,8},{10,11... | collective-permute-start | bytes 1179656 | tf_op jit(solution)/shard_map/ppermute | solution.py:209
  55.1 50.9 %collective-permute-start.14 = (bf16[384,768]{1,0:T(8,128)(2,1)S(1)}, bf16[384,768]{1,0:T(8,128)(2,1)S(1)}, u32[]{:S(2)}, u32[]{:S(2)}) collective-permute-start(bf16[384,768]{1,0:T(8,128)(2,1)S(1)} %shard_map.132.refs_0_), channel_id=1, source_target_pairs={{0,1},{1,0},{2,3},{3,2},{4,5},{5,4},{6,7},{7,6},{8,9},{9,8},{10,11... | collective-permute-start | bytes 1769480 | tf_op jit(solution)/shard_map/ppermute | solution.py:319
  62.6 20.1 %collective-permute-start.16 = (bf16[256,768]{1,0:T(8,128)(2,1)S(1)}, bf16[256,768]{1,0:T(8,128)(2,1)S(1)}, u32[]{:S(2)}, u32[]{:S(2)}) collective-permute-start(bf16[256,768]{1,0:T(8,128)(2,1)S(1)} %get-tuple-element.58), channel_id=1, source_target_pairs={{0,2},{1,3},{2,0},{3,1},{4,6},{5,7},{6,4},{7,5},{8,10},{9,11},{10,... | collective-permute-start | bytes 1179656 | tf_op jit(solution)/shard_map/ppermute | solution.py:209
  75.8 21.4 %collective-permute-start.18 = (bf16[256,768]{1,0:T(8,128)(2,1)S(1)}, bf16[256,768]{1,0:T(8,128)(2,1)S(1)}, u32[]{:S(2)}, u32[]{:S(2)}) collective-permute-start(bf16[256,768]{1,0:T(8,128)(2,1)S(1)} %get-tuple-element.60), channel_id=1, source_target_pairs={{0,4},{1,5},{6,2},{7,3},{8,12},{9,13},{14,10},{15,11},{16,20},{17,... | collective-permute-start | bytes 1179656 | tf_op jit(solution)/shard_map/ppermute | solution.py:209
  79.6 25.1 %collective-permute-start.21 = (bf16[256,768]{1,0:T(8,128)(2,1)S(1)}, bf16[256,768]{1,0:T(8,128)(2,1)S(1)}, u32[]{:S(2)}, u32[]{:S(2)}) collective-permute-start(bf16[256,768]{1,0:T(8,128)(2,1)S(1)} %get-tuple-element.62), channel_id=1, source_target_pairs={{0,5},{1,4},{6,3},{7,2},{8,13},{9,12},{14,11},{15,10},{16,21},{17,... | collective-permute-start | bytes 1179656 | tf_op jit(solution)/shard_map/ppermute | solution.py:209
  82.7 32.6 %collective-permute-start.23 = (bf16[256,768]{1,0:T(8,128)(2,1)S(1)}, bf16[256,768]{1,0:T(8,128)(2,1)S(1)}, u32[]{:S(2)}, u32[]{:S(2)}) collective-permute-start(bf16[256,768]{1,0:T(8,128)(2,1)S(1)} %get-tuple-element.64), channel_id=1, source_target_pairs={{0,6},{1,7},{6,0},{7,1},{8,14},{9,15},{14,8},{15,9},{16,22},{17,23... | collective-permute-start | bytes 1179656 | tf_op jit(solution)/shard_map/ppermute | solution.py:209
  91.2 35.0 %collective-permute-start.25 = (bf16[256,768]{1,0:T(8,128)(2,1)S(1)}, bf16[256,768]{1,0:T(8,128)(2,1)S(1)}, u32[]{:S(2)}, u32[]{:S(2)}) collective-permute-start(bf16[256,768]{1,0:T(8,128)(2,1)S(1)} %get-tuple-element.66), channel_id=1, source_target_pairs={{0,7},{1,6},{6,1},{7,0},{8,15},{9,14},{14,9},{15,8},{16,23},{17,22... | collective-permute-start | bytes 1179656 | tf_op jit(solution)/shard_map/ppermute | solution.py:209
  97.2 29.0 %collective-permute-start.20 = (bf16[256,768]{1,0:T(8,128)(2,1)S(1)}, bf16[256,768]{1,0:T(8,128)(2,1)S(1)}, u32[]{:S(2)}, u32[]{:S(2)}) collective-permute-start(bf16[256,768]{1,0:T(8,128)(2,1)S(1)} %get-tuple-element.61), channel_id=1, source_target_pairs={{2,0},{3,1},{4,6},{5,7},{10,8},{11,9},{12,14},{13,15},{18,16},{19,... | collective-permute-start | bytes 1179656 | tf_op jit(solution)/shard_map/ppermute | solution.py:209
  104.7 31.6 %collective-permute-start.22 = (bf16[256,768]{1,0:T(8,128)(2,1)S(1)}, bf16[256,768]{1,0:T(8,128)(2,1)S(1)}, u32[]{:S(2)}, u32[]{:S(2)}) collective-permute-start(bf16[256,768]{1,0:T(8,128)(2,1)S(1)} %get-tuple-element.63), channel_id=1, source_target_pairs={{2,1},{3,0},{4,7},{5,6},{10,9},{11,8},{12,15},{13,14},{18,17},{19,... | collective-permute-start | bytes 1179656 | tf_op jit(solution)/shard_map/ppermute | solution.py:209
  106.0 30.2 %collective-permute-start.24 = (bf16[256,768]{1,0:T(8,128)(2,1)S(1)}, bf16[256,768]{1,0:T(8,128)(2,1)S(1)}, u32[]{:S(2)}, u32[]{:S(2)}) collective-permute-start(bf16[256,768]{1,0:T(8,128)(2,1)S(1)} %get-tuple-element.65), channel_id=1, source_target_pairs={{2,3},{3,2},{4,5},{5,4},{10,11},{11,10},{12,13},{13,12},{18,19},{1... | collective-permute-start | bytes 1179656 | tf_op jit(solution)/shard_map/ppermute | solution.py:209
  163.4 42.2 %collective-permute-start.44 = (bf16[512,768]{1,0:T(8,128)(2,1)S(1)}, bf16[512,768]{1,0:T(8,128)(2,1)S(1)}, u32[]{:S(2)}, u32[]{:S(2)}) collective-permute-start(bf16[512,768]{1,0:T(8,128)(2,1)S(1)} %get-tuple-element.67.back), channel_id=1, source_target_pairs={{2,4},{3,5},{4,2},{5,3},{10,12},{11,13},{12,10},{13,11},{18,20},{1... | collective-permute-start | bytes 2359304 | tf_op jit(solution)/shard_map/ppermute | solution.py:209
  164.3 21.6 %collective-permute-start.26 = (bf16[256,768]{1,0:T(8,128)(2,1)S(1)}, bf16[256,768]{1,0:T(8,128)(2,1)S(1)}, u32[]{:S(2)}, u32[]{:S(2)}) collective-permute-start(bf16[256,768]{1,0:T(8,128)(2,1)S(1)} %get-tuple-element.69), channel_id=1, source_target_pairs={{0,8},{8,16},{16,24},{24,0},{1,9},{9,17},{17,25},{25,1},{2,10},{10... | collective-permute-start | bytes 1179656 | tf_op jit(solution)/shard_map/ppermute | solution.py:243
  179.1 19.8 %collective-permute-start.27 = (bf16[256,768]{1,0:T(8,128)(2,1)S(1)}, bf16[256,768]{1,0:T(8,128)(2,1)S(1)}, u32[]{:S(2)}, u32[]{:S(2)}) collective-permute-start(bf16[256,768]{1,0:T(8,128)(2,1)S(1)} %get-tuple-element.70), channel_id=1, source_target_pairs={{0,16},{8,24},{16,0},{24,8},{1,17},{9,25},{17,1},{25,9},{2,18},{10... | collective-permute-start | bytes 1179656 | tf_op jit(solution)/shard_map/ppermute | solution.py:243
  185.9 46.0 %collective-permute-start.39 = (bf16[384,768]{1,0:T(8,128)(2,1)S(1)}, bf16[384,768]{1,0:T(8,128)(2,1)S(1)}, u32[]{:S(2)}, u32[]{:S(2)}) collective-permute-start(bf16[384,768]{1,0:T(8,128)(2,1)S(1)} %shard_map.136.refs_0_), channel_id=1, source_target_pairs={{0,1},{1,0},{2,3},{3,2},{4,5},{5,4},{6,7},{7,6},{8,9},{9,8},{10,11... | collective-permute-start | bytes 1769480 | tf_op jit(solution)/shard_map/ppermute | solution.py:319
  202.9 20.3 %collective-permute-start.43 = (bf16[256,768]{1,0:T(8,128)(2,1)S(1)}, bf16[256,768]{1,0:T(8,128)(2,1)S(1)}, u32[]{:S(2)}, u32[]{:S(2)}) collective-permute-start(bf16[256,768]{1,0:T(8,128)(2,1)S(1)} %get-tuple-element.82), channel_id=1, source_target_pairs={{0,4},{1,5},{6,2},{7,3},{8,12},{9,13},{14,10},{15,11},{16,20},{17,... | collective-permute-start | bytes 1179656 | tf_op jit(solution)/shard_map/ppermute | solution.py:209
  205.6 24.9 %collective-permute-start.46 = (bf16[256,768]{1,0:T(8,128)(2,1)S(1)}, bf16[256,768]{1,0:T(8,128)(2,1)S(1)}, u32[]{:S(2)}, u32[]{:S(2)}) collective-permute-start(bf16[256,768]{1,0:T(8,128)(2,1)S(1)} %get-tuple-element.84), channel_id=1, source_target_pairs={{0,5},{1,4},{6,3},{7,2},{8,13},{9,12},{14,11},{15,10},{16,21},{17,... | collective-permute-start | bytes 1179656 | tf_op jit(solution)/shard_map/ppermute | solution.py:209
  208.4 33.6 %collective-permute-start.48 = (bf16[256,768]{1,0:T(8,128)(2,1)S(1)}, bf16[256,768]{1,0:T(8,128)(2,1)S(1)}, u32[]{:S(2)}, u32[]{:S(2)}) collective-permute-start(bf16[256,768]{1,0:T(8,128)(2,1)S(1)} %get-tuple-element.86), channel_id=1, source_target_pairs={{0,6},{1,7},{6,0},{7,1},{8,14},{9,15},{14,8},{15,9},{16,22},{17,23... | collective-permute-start | bytes 1179656 | tf_op jit(solution)/shard_map/ppermute | solution.py:209
  218.2 34.6 %collective-permute-start.50 = (bf16[256,768]{1,0:T(8,128)(2,1)S(1)}, bf16[256,768]{1,0:T(8,128)(2,1)S(1)}, u32[]{:S(2)}, u32[]{:S(2)}) collective-permute-start(bf16[256,768]{1,0:T(8,128)(2,1)S(1)} %get-tuple-element.88), channel_id=1, source_target_pairs={{0,7},{1,6},{6,1},{7,0},{8,15},{9,14},{14,9},{15,8},{16,23},{17,22... | collective-permute-start | bytes 1179656 | tf_op jit(solution)/shard_map/ppermute | solution.py:209
  223.3 29.5 %collective-permute-start.45 = (bf16[256,768]{1,0:T(8,128)(2,1)S(1)}, bf16[256,768]{1,0:T(8,128)(2,1)S(1)}, u32[]{:S(2)}, u32[]{:S(2)}) collective-permute-start(bf16[256,768]{1,0:T(8,128)(2,1)S(1)} %get-tuple-element.83), channel_id=1, source_target_pairs={{2,0},{3,1},{4,6},{5,7},{10,8},{11,9},{12,14},{13,15},{18,16},{19,... | collective-permute-start | bytes 1179656 | tf_op jit(solution)/shard_map/ppermute | solution.py:209
  230.6 32.2 %collective-permute-start.47 = (bf16[256,768]{1,0:T(8,128)(2,1)S(1)}, bf16[256,768]{1,0:T(8,128)(2,1)S(1)}, u32[]{:S(2)}, u32[]{:S(2)}) collective-permute-start(bf16[256,768]{1,0:T(8,128)(2,1)S(1)} %get-tuple-element.85), channel_id=1, source_target_pairs={{2,1},{3,0},{4,7},{5,6},{10,9},{11,8},{12,15},{13,14},{18,17},{19,... | collective-permute-start | bytes 1179656 | tf_op jit(solution)/shard_map/ppermute | solution.py:209
  231.9 30.9 %collective-permute-start.49 = (bf16[256,768]{1,0:T(8,128)(2,1)S(1)}, bf16[256,768]{1,0:T(8,128)(2,1)S(1)}, u32[]{:S(2)}, u32[]{:S(2)}) collective-permute-start(bf16[256,768]{1,0:T(8,128)(2,1)S(1)} %get-tuple-element.87), channel_id=1, source_target_pairs={{2,3},{3,2},{4,5},{5,4},{10,11},{11,10},{12,13},{13,12},{18,19},{1... | collective-permute-start | bytes 1179656 | tf_op jit(solution)/shard_map/ppermute | solution.py:209
  (41 other events, 458.3 us)

commit v2 on v1

--- a/solution.py
+++ b/solution.py
@@ -30,38 +30,45 @@
     return lax.dot_general(left, weight, (((1,), (1,)), ((), ())), preferred_element_type=F32)
 
 
-def start_sends(back, send_group, send_member, group_outs, member_outs, sems, rows):
+def start_sends(back, ready, send_group, send_member, outs, cross, sems, rows):
     members, capacity = send_member.shape[1], send_member.shape[2]
     own_group, own_member = lax.axis_index("group"), lax.axis_index("member")
+    source = back.at[pl.ds(ready * rows, rows), :]
     copies = []
-
-    def send(block, out):
-        source = back.at[pl.ds(pl.multiple_of(block * rows, rows), rows), :]
-        copies.append(pltpu.make_async_copy(source, out, sems.at[len(copies)]))
-        copies[-1].start()
-
-    for place, out in enumerate(group_outs):
-        send(send_group[0, own_group ^ (place + 1)], out)
-    for place, out in enumerate(member_outs):
-        shift, which = 1 + place // capacity, place % capacity
-        send(send_member[0, lax.rem(own_member + shift, members), which], out)
+    for number, out in enumerate(outs):
+        if number < cross:
+            block = send_group[0, own_group ^ (number + 1)]
+        else:
+            shift, which = 1 + (number - cross) // capacity, (number - cross) % capacity
+            block = send_member[0, lax.rem(own_member + shift, members), which]
+        copies.append(pltpu.make_async_copy(source, out, sems.at[number]))
+
+        @pl.when(block == ready)
+        def _():
+            copies[-1].start()
+
     return copies
 
 
 def first_kernel(rows, cross, send_group, send_member, agg, weight, grad, pull_out, back_out, *rest):
     *outs, sems = rest
-    for start in range(0, agg.shape[0], rows):
-        part = pl.ds(start, rows)
+    copies = []
+    for block in range(agg.shape[0] // rows):
+        part = pl.ds(block * rows, rows)
         lift = jnp.dot(agg[part, :], weight[...], preferred_element_type=F32)
         pull = (grad[part, :].astype(F32) * silu_slope(lift)).astype(BF16)
         pull_out[part, :] = pull
         back_out[part, :] = times_transpose(pull, weight[...]).astype(BF16)
-    for copy in start_sends(back_out, send_group, send_member, outs[:cross], outs[cross:], sems, rows):
+        copies = start_sends(back_out, block, send_group, send_member, outs, cross, sems, rows)
+    for copy in copies:
         copy.wait()
 
 
-def sweep_kernel(rows, cross, src_slot, dst_block, block_count, send_member, back, base, values, *rest):
-    *received, total, pool, sems = rest
+def sweep_kernel(
+    rows, groups, places, plan, src_slot, dst_block, block_count, send_member, far_table, back, base, values, *rest
+):
+    early, rest = split_received(plan, rest)
+    *received, total, pool, held, blocks, sems, early_sems = rest
     members, capacity = send_member.shape[1], send_member.shape[2]
     local = back.shape[0] // rows
     own = lax.axis_index("member")
@@ -80,6 +87,7 @@
         shift, which = 1 + place // capacity, place % capacity
         peer = lax.rem(own + (members - shift), members)
         fill(source, local + peer * capacity + which)
+    loads = fetch_cross(rows, groups, places, far_table, early, blocks, values, held, early_sems)
     total[...] = base[...].astype(F32).reshape(total.shape)
     for copy in copies:
         copy.wait()
@@ -88,7 +96,8 @@
         total[dst_block[0, slot]] += turned_dot(values[slot], pool[src_slot[0, slot]])
         return carry
 
-    lax.fori_loop(cross, block_count[0], step, 0)
+    lax.fori_loop(groups - 1, block_count[0], step, 0)
+    add_cross(groups, places, total, dst_block, held, blocks, loads)
 
 
 def is_inner(groups):
@@ -96,47 +105,44 @@
     return (chip > 0) & (chip < groups // PAIR - 1)
 
 
-def fetch_cross(rows, groups, far_table, received, blocks, values, held, sems):
+def slot_of(place, groups):
+    own = lax.axis_index("group")
+    return lax.rem((own ^ (place + 1)) + (groups - 1 - own), groups)
+
+
+def fetch_cross(rows, groups, places, far_table, received, blocks, values, held, sems):
     own = lax.axis_index("group")
     loads = []
-
-    def load(source, to):
-        copy = pltpu.make_async_copy(source, to, sems.at[len(loads)])
-        loads.append(copy)
-        return copy
-
-    for place, sources in enumerate(received):
-        slot = lax.rem((own ^ (place + 1)) + (groups - 1 - own), groups)
-        load(values.at[slot], held.at[place]).start()
+    for number, (place, sources) in enumerate(zip(places, received)):
+        value_sem, block_sem, to = sems.at[2 * number], sems.at[2 * number + 1], blocks.at[number]
+        loads.append(pltpu.make_async_copy(values.at[slot_of(place, groups)], held.at[number], value_sem))
+        loads[-1].start()
+        loads.append(pltpu.make_async_copy(sources[-1], to, block_sem))
         if len(sources) == 1:
-            load(sources[0], blocks.at[place]).start()
+            loads[-1].start()
             continue
-        inner, outer = sources
+        inner = sources[0]
         if inner.shape[0] != rows:
             picked = pl.multiple_of(far_table[0, own] * rows, rows)
             inner = inner.at[pl.ds(picked, rows), :]
-        near = pltpu.make_async_copy(inner, blocks.at[place], sems.at[len(loads)])
-        copy = load(outer, blocks.at[place])
         deep = is_inner(groups)
 
         @pl.when(deep)
         def _():
-            near.start()
+            pltpu.make_async_copy(inner, to, block_sem).start()
 
         @pl.when(jnp.logical_not(deep))
         def _():
-            copy.start()
+            loads[-1].start()
 
     return loads
 
 
-def add_cross(groups, total, dst_block, held, blocks, loads):
-    own = lax.axis_index("group")
-    for place in range(groups - 1):
-        slot = lax.rem((own ^ (place + 1)) + (groups - 1 - own), groups)
-        loads[2 * place].wait()
-        loads[2 * place + 1].wait()
-        total[dst_block[0, slot]] += turned_dot(held[place], blocks[place])
+def add_cross(groups, places, total, dst_block, held, blocks, loads):
+    for number, place in enumerate(places):
+        loads[2 * number].wait()
+        loads[2 * number + 1].wait()
+        total[dst_block[0, slot_of(place, groups)]] += turned_dot(held[number], blocks[number])
 
 
 def split_received(plan, refs):
@@ -161,28 +167,32 @@
 
 
 def middle_kernel(
-    rows, plan, send_group, send_member, dst_block, far_table, base, slope, weight, values, after, *rest
+    rows, groups, places, plan, send_group, send_member, dst_block, far_table, base, slope, weight, values, *rest
 ):
     received, rest = split_received(plan, rest)
-    cross = len(plan)
     carry_out, pull_out, back_out, *outs, held, blocks, sems, send_sems = rest
-    loads = fetch_cross(rows, cross + 1, far_table, received, blocks, values, held, sems)
+    loads = fetch_cross(rows, groups, places, far_table, received, blocks, values, held, sems)
     carry_out[...] = base[...]
-    add_cross(cross + 1, carry_out, dst_block, held, blocks, loads)
+    add_cross(groups, places, carry_out, dst_block, held, blocks, loads)
+    copies = []
     for block in range(carry_out.shape[0]):
         part = pl.ds(block * rows, rows)
         pull = (carry_out[block] * slope[part, :]).astype(BF16)
         pull_out[part, :] = pull
         back_out[part, :] = times_transpose(pull, weight[...]).astype(BF16)
-    for copy in start_sends(back_out, send_group, send_member, outs[:cross], outs[cross:], send_sems, rows):
+        copies = start_sends(back_out, block, send_group, send_member, outs, groups - 1, send_sems, rows)
+    for copy in copies:
         copy.wait()
 
 
-def last_kernel(rows, plan, dst_block, far_table, base, values, after, *rest):
-    received, (out, total, held, blocks, sems) = split_received(plan, rest)
-    loads = fetch_cross(rows, len(plan) + 1, far_table, received, blocks, values, held, sems)
+def last_kernel(
+    rows, groups, places, plan, scale, dst_block, far_table, base, own_half, sibling_half, values, after, *rest
+):
+    received, (out, grad, total, held, blocks, sems) = split_received(plan, rest)
+    loads = fetch_cross(rows, groups, places, far_table, received, blocks, values, held, sems)
     total[...] = base[...]
-    add_cross(len(plan) + 1, total, dst_block, held, blocks, loads)
+    finish_kernel(scale, own_half, sibling_half, grad)
+    add_cross(groups, places, total, dst_block, held, blocks, loads)
     out[...] = total[...].reshape(out.shape).astype(BF16)
 
 
@@ -307,31 +317,34 @@
     return parts[0]
 
 
-def weight_total(aggregate, pulled, scale):
+def stage(blocks, axis, stride, size):
+    _, perms = stage_peers(axis, stride, size)
+    return [lax.ppermute(block, axis, perm) for block, perm in zip(blocks, perms)]
+
+
+def weight_piece(aggregate, pulled):
     groups, members = lax.axis_size("group"), lax.axis_size("member")
     width, depth = aggregate.shape[1], pulled.shape[1]
     half, piece = width // PAIR, width // PAIR // members
-    _, pair_perms = stage_peers("group", 1, PAIR)
-    _, member_perms = stage_peers("member", 1, members)
-    _, line_perms = stage_peers("group", PAIR, groups // PAIR)
-
-    def permute(blocks, axis, perms):
-        return [lax.ppermute(block, axis, perm) for block, perm in zip(blocks, perms)]
 
     def shape(rows, dtype):
         return jax.ShapeDtypeStruct((rows, depth), dtype)
 
     keep, give = kernel_call(part_kernel, [shape(half, F32), shape(half, BF16)], (aggregate, pulled))
-    (got,) = permute([give], "group", pair_perms)
+    (got,) = stage([give], "group", 1, PAIR)
     own, *gives = kernel_call(split_kernel, [shape(piece, F32)] + [shape(piece, BF16)] * (members - 1), (keep, got))
-    got = permute(gives, "member", member_perms)
+    got = stage(gives, "member", 1, members)
     total = sum((block.astype(F32) for block in got), own).astype(BF16)
-    got = permute([total] * (groups // PAIR - 1), "group", line_perms)
-    total = pairwise([block.astype(F32) for block in [total] + got]).astype(BF16)
-    got = permute([total] * (members - 1), "member", member_perms)
-    total = kernel_call(join_kernel, shape(half, BF16), [total] + got)
-    got = permute([total], "group", pair_perms)
-    return kernel_call(functools.partial(finish_kernel, scale), shape(width, F32), [total] + got)
+    got = stage([total] * (groups // PAIR - 1), "group", PAIR, groups // PAIR)
+    return pairwise([block.astype(F32) for block in [total] + got]).astype(BF16)
+
+
+def weight_halves(total):
+    members = lax.axis_size("member")
+    got = stage([total] * (members - 1), "member", 1, members)
+    shape = jax.ShapeDtypeStruct((members * total.shape[0], total.shape[1]), BF16)
+    half = kernel_call(join_kernel, shape, [total] + got)
+    return [half] + stage([half], "group", 1, PAIR)
 
 
 def body(
@@ -358,29 +371,43 @@
 
     field = jax.ShapeDtypeStruct((labels, width), BF16)
     total = jax.ShapeDtypeStruct((local, rows, width), F32)
+    square = jax.ShapeDtypeStruct(hop_one_weight.shape, F32)
     sends = send_shapes(rows, width, cross + peers)
     send_sems = pltpu.SemaphoreType.DMA((cross + peers,))
-    cross_scratch = [
-        pltpu.VMEM((cross, rows, rows), BF16),
-        pltpu.VMEM((cross, rows, width), BF16),
-    ]
-
-    def sweep(back, base, received):
+    plan = [1, 1, 1, 2, 2, 2, 2] if relayed(groups) else [1] * cross
+    late = (3, 4) if relayed(groups) else tuple(range(cross))
+    early = tuple(place for place in range(cross) if place not in late)
+    early_plan, late_plan = [plan[place] for place in early], [plan[place] for place in late]
+
+    def cross_scratch(places):
+        count = max(len(places), 1)
+        return [
+            pltpu.VMEM((count, rows, rows), BF16),
+            pltpu.VMEM((count, rows, width), BF16),
+        ], pltpu.SemaphoreType.DMA((2 * count,))
+
+    def pick(blocks, places):
+        return sum((blocks[place] for place in places), [])
+
+    def sweep(back, base, from_group, received):
+        scratch, sems = cross_scratch(early)
         return pl.pallas_call(
-            functools.partial(sweep_kernel, rows, cross),
+            functools.partial(sweep_kernel, rows, groups, early, early_plan),
             out_shape=total,
-            in_specs=[SMEM, SMEM, SMEM, SMEM, ANY, VMEM, VMEM] + [ANY] * peers,
+            in_specs=[SMEM] * 5 + [ANY] + [VMEM] * 2 + [ANY] * (sum(early_plan) + peers),
             out_specs=VMEM,
-            scratch_shapes=[
-                pltpu.VMEM((local + members * capacity, rows, width), BF16),
-                pltpu.SemaphoreType.DMA((local + members * capacity,)),
-            ],
+            scratch_shapes=[pltpu.VMEM((local + members * capacity, rows, width), BF16)]
+            + scratch
+            + [pltpu.SemaphoreType.DMA((local + members * capacity,)), sems],
             compiler_params=params(),
             name="sweep",
-        )(src_slot, dst_block, block_count, send_member, back, base, block_values, *received)
-
-    plan = [1, 1, 1, 2, 2, 2, 2] if relayed(groups) else [1] * cross
-
+        )(
+            *(src_slot, dst_block, block_count, send_member, far_table, back, base, block_values),
+            *pick(from_group, early),
+            *received,
+        )
+
+    scratch, sems = cross_scratch(late)
     far_table = send_group
     if relayed(groups):
         far_table = lax.ppermute(send_group, "group", [(g, g ^ 6) for g in range(groups)])
@@ -396,38 +423,38 @@
     from_group = group_exchange(rows, back_two, outs[:cross], far_table)
     from_member = member_exchange(outs[cross:], capacity)
     slope_one = silu_slope(jnp.dot(agg_one, hop_one_weight, preferred_element_type=F32))
-    grad_w_two = weight_total(agg_two, pull_two, grad_scale)
-    base_two = sweep(back_two, grad_out, from_member)
-
+    piece_two = weight_piece(agg_two, pull_two)
+    base_two = sweep(back_two, grad_out, from_group, from_member)
     carry, pull_one, back_one, *outs = pl.pallas_call(
-        functools.partial(middle_kernel, rows, plan),
+        functools.partial(middle_kernel, rows, groups, late, late_plan),
         out_shape=[total, field, field] + sends,
-        in_specs=[SMEM] * 4 + [VMEM] * 3 + [ANY] * (2 + sum(plan)),
+        in_specs=[SMEM] * 4 + [VMEM] * 3 + [ANY] * (1 + sum(late_plan)),
         out_specs=[VMEM, VMEM, VMEM] + [ANY] * (cross + peers),
-        scratch_shapes=cross_scratch + [pltpu.SemaphoreType.DMA((2 * cross,)), send_sems],
+        scratch_shapes=scratch + [sems, send_sems],
         compiler_params=params(),
         name="middle",
     )(
         *(send_group, send_member, dst_block, far_table, base_two, slope_one),
-        *(hop_one_weight, block_values, grad_w_two),
-        *sum(from_group, []),
+        *(hop_one_weight, block_values),
+        *pick(from_group, late),
     )
+
     from_group = group_exchange(rows, back_one, outs[:cross], far_table)
     from_member = member_exchange(outs[cross:], capacity)
-    grad_w_one = weight_total(agg_one, pull_one, grad_scale)
-    base_one = sweep(back_one, carry, from_member)
-
-    grad_emb = pl.pallas_call(
-        functools.partial(last_kernel, rows, plan),
-        out_shape=field,
-        in_specs=[SMEM] * 2 + [VMEM] + [ANY] * (2 + sum(plan)),
-        out_specs=VMEM,
-        scratch_shapes=[pltpu.VMEM((local, rows, width), F32)]
-        + cross_scratch
-        + [pltpu.SemaphoreType.DMA((2 * cross,))],
+    halves_two = weight_halves(piece_two)
+    halves_one = weight_halves(weight_piece(agg_one, pull_one))
+    base_one = sweep(back_one, carry, from_group, from_member)
+    grad_w_two = kernel_call(functools.partial(finish_kernel, grad_scale), square, halves_two)
+
+    grad_emb, grad_w_one = pl.pallas_call(
+        functools.partial(last_kernel, rows, groups, late, late_plan, grad_scale),
+        out_shape=[field, square],
+        in_specs=[SMEM] * 2 + [VMEM] * 3 + [ANY] * (2 + sum(late_plan)),
+        out_specs=[VMEM, VMEM],
+        scratch_shapes=[pltpu.VMEM((local, rows, width), F32)] + scratch + [sems],
         compiler_params=params(),
         name="last",
-    )(dst_block, far_table, base_one, block_values, grad_w_one, *sum(from_group, []))
+    )(dst_block, far_table, base_one, *halves_one, block_values, grad_w_two, *pick(from_group, late))
     return (grad_emb, grad_w_one, grad_w_two)
 
 

time: 272 us -> 242 us (0.89)
  waiting for transfers between devices: 136 us -> 94 us
  starting transfers between devices: 85.2 us -> 102 us
  local copies, waits for them, and re-layouts: 9.2 us -> 5.16 us
    ppermute x22, starting transfers between devices: 19.1 us -> 42 us  [stage(): lax.ppermute(block, axis, perm)]
    ppermute x22, waiting for transfers between devices: 68.2 us -> 46 us  [permute(): lax.ppermute(block, 'group', [(g, g ^ peer) for g in range(groups) if kee...]
    ppermute x22, waiting for transfers between devices: 44.2 us -> 29.5 us  [stage(): lax.ppermute(block, axis, perm)]
    ppermute x22, starting transfers between devices: 61.5 us -> 50.1 us  [permute(): lax.ppermute(block, 'group', [(g, g ^ peer) for g in range(groups) if kee...]
    ppermute x6, waiting for transfers between devices: 20.4 us -> 11.5 us  [member_exchange(): lax.ppermute(block, 'member', [(m, (m + 1 + place // capacity) % members)...]
    ppermute x6, starting transfers between devices: 3.26 us -> 8.39 us  [member_exchange(): lax.ppermute(block, 'member', [(m, (m + 1 + place // capacity) % members)...]
    ppermute x1, waiting for transfers between devices: 2.91 us -> 7.08 us  [body(): lax.ppermute(send_group, 'group', [(g, g ^ 6) for g in range(groups)])]
    unnamed x29 -> x25, local copies, waits for them, and re-layouts: 9.2 us -> 5.16 us
  transfers between devices with their start and end apart: 51 -> 51, of which waited for: 28 -> 18; matrix products, arithmetic and copies ran while one was open for 0% -> 1% of each run, Pallas kernels for 6% -> 12%
where the time goes in v2:
time: 242 us
  starting transfers between devices  102 us (42%)
  waiting for transfers between devices  94 us (39%)
  Pallas kernels  37.7 us (16%)
  local copies, waits for them, and re-layouts  5.16 us (2%)
    ppermute x22, starting transfers between devices, permute(): lax.ppermute(block, 'group', [(g, g ^ peer) for g in range(groups) if kee...  50.1 us
    ppermute x22, waiting for transfers between devices, permute(): lax.ppermute(block, 'group', [(g, g ^ peer) for g in range(groups) if kee...  46 us
    ppermute x22, starting transfers between devices, stage(): lax.ppermute(block, axis, perm)  42 us
    ppermute x22, waiting for transfers between devices, stage(): lax.ppermute(block, axis, perm)  29.5 us
    pallas_call x2, Pallas kernels, sweep(): pl.pallas_call(functools.partial(sweep_kernel, rows, groups, early, early...  16.9 us
    ppermute x6, waiting for transfers between devices, member_exchange(): lax.ppermute(block, 'member', [(m, (m + 1 + place // capacity) % members)...  11.5 us
    ppermute x6, starting transfers between devices, member_exchange(): lax.ppermute(block, 'member', [(m, (m + 1 + place // capacity) % members)...  8.39 us
    ppermute x1, waiting for transfers between devices, body(): lax.ppermute(send_group, 'group', [(g, g ^ 6) for g in range(groups)])  7.08 us
  transfers between devices with their start and end apart: 51, of which 18 were waited for; matrix products, arithmetic and copies ran while one was open for 1% of the time, Pallas kernels for 12%

profile of v2, /device:TPU:3, one launch (start us, length us, event | category | flops | bytes accessed | tf_op | source)
XLA Modules:
  0.0 241.8 jit_solution(9437953274485882048)
XLA Ops:
  5.6 4.6 %first.1 = (bf16[512,768]{1,0:T(8,128)(2,1)S(1)}, bf16[512,768]{1,0:T(8,128)(2,1)S(1)}, bf16[256,768]{1,0:T(8,128)(2,1)S(1)}, bf16[256,768]{1,0:T(8,128)(2,1)S(1...) custom-call(s32[1,8]{1,0:T(1,128)S(1)} %copy-done.10, ...), custom_call_target="tpu_custom_call" | custom-call | tf_op jit(solution)/shard_map/first/pallas_call | solution.py:414
  11.6 4.1 %collective-permute-start.2 = (bf16[256,768]{1,0:T(8,128)(2,1)S(1)}, bf16[256,768]{1,0:T(8,128)(2,1)S(1)}, u32[]{:S(2)}, u32[]{:S(2)}) collective-permute-start(bf16[256,768]{1,0:T(8,128)(2,1)S(1)} %get-tuple-element.50), channel_id=1, source_target_pairs={{0,2},{1,3},{2,0},{3,1},{4,6},{5,7},{6,4},{7,5},{8,10},{9,11},{10,... | collective-permute-start | bytes 1179656 | tf_op jit(solution)/shard_map/ppermute | solution.py:219
  18.5 7.1 %collective-permute-done.far_table = s32[1,8]{1,0:T(1,128)S(1)} collective-permute-done((s32[1,8]{1,0:T(1,128)S(1)}, s32[1,8]{1,0:T(1,128)S(1)}, u32[]{:S(2)}, u32[]{:S(2)}) %collective-permute-start) | collective-permute-done | bytes 64 | tf_op jit(solution)/shard_map/ppermute | solution.py:413
  25.6 7.7 %collective-permute-start.3 = (bf16[256,768]{1,0:T(8,128)(2,1)S(1)}, bf16[256,768]{1,0:T(8,128)(2,1)S(1)}, u32[]{:S(2)}, u32[]{:S(2)}) collective-permute-start(bf16[256,768]{1,0:T(8,128)(2,1)S(1)} %get-tuple-element.51), channel_id=1, source_target_pairs={{0,3},{1,2},{2,1},{3,0},{4,7},{5,6},{6,5},{7,4},{8,11},{9,10},{10,... | collective-permute-start | bytes 1179656 | tf_op jit(solution)/shard_map/ppermute | solution.py:219
  33.3 4.1 %collective-permute-start.5 = (bf16[256,768]{1,0:T(8,128)(2,1)S(1)}, bf16[256,768]{1,0:T(8,128)(2,1)S(1)}, u32[]{:S(2)}, u32[]{:S(2)}) collective-permute-start(bf16[256,768]{1,0:T(8,128)(2,1)S(1)} %get-tuple-element.52), channel_id=1, source_target_pairs={{0,6},{1,7},{6,0},{7,1},{8,14},{9,15},{14,8},{15,9},{16,22},{17,23... | collective-permute-start | bytes 1179656 | tf_op jit(solution)/shard_map/ppermute | solution.py:219
  43.5 9.8 %collective-permute-done.5.rest_4_ = bf16[256,768]{1,0:T(8,128)(2,1)S(1)} collective-permute-done((bf16[256,768]{1,0:T(8,128)(2,1)S(1)}, bf16[256,768]{1,0:T(8,128)(2,1)S(1)}, u32[]{:S(2)}, u32[]{:S(2)}) %collective-permute-start.5) | collective-permute-done | bytes 393248 | tf_op jit(solution)/shard_map/ppermute | solution.py:219
  53.5 6.6 %collective-permute-done.7.rest_6_ = bf16[256,768]{1,0:T(8,128)(2,1)S(1)} collective-permute-done((bf16[256,768]{1,0:T(8,128)(2,1)S(1)}, bf16[256,768]{1,0:T(8,128)(2,1)S(1)}, u32[]{:S(2)}, u32[]{:S(2)}) %collective-permute-start.7) | collective-permute-done | bytes 393248 | tf_op jit(solution)/shard_map/ppermute | solution.py:219
  69.1 8.2 %collective-permute-done.13.rest_2_ = bf16[256,768]{1,0:T(8,128)(2,1)S(1)} collective-permute-done((bf16[256,768]{1,0:T(8,128)(2,1)S(1)}, bf16[256,768]{1,0:T(8,128)(2,1)S(1)}, u32[]{:S(2)}, u32[]{:S(2)}) %collective-permute-start.13) | collective-permute-done | bytes 393248 | tf_op jit(solution)/shard_map/ppermute | solution.py:219
  82.0 8.5 %sweep.2.base = f32[2,256,768]{2,1,0:T(8,128)S(1)} custom-call(s32[1,24]{1,0:T(1,128)S(1)} %copy-done.11, s32[1,24]{1,0:T(1,128)S(1)} %copy-done.9, s32[1]{0:T(128)S(6)} %copy.18.block_count, s32[1,4,1]{2,1,0:T(4,128)S(1)} %copy.17.send_member, s32[1,8]{1,0:T(1,128)S(1)} %collective-permute-done.far_table, bf16[512,768]{1,0:T(8,128)(2,1)S(1)} %get-tuple-element.48.back, ...), custom_call_target="tpu_custom_call" | custom-call | tf_op jit(solution)/shard_map/sweep/pallas_call | solution.py:394
  90.5 9.2 %collective-permute-done.14.rest_3_ = bf16[256,768]{1,0:T(8,128)(2,1)S(1)} collective-permute-done((bf16[256,768]{1,0:T(8,128)(2,1)S(1)}, bf16[256,768]{1,0:T(8,128)(2,1)S(1)}, u32[]{:S(2)}, u32[]{:S(2)}) %collective-permute-start.14) | collective-permute-done | bytes 393248 | tf_op jit(solution)/shard_map/ppermute | solution.py:219
  99.6 5.6 %middle.1 = (f32[2,256,768]{2,1,0:T(8,128)S(1)}, bf16[512,768]{1,0:T(8,128)(2,1)S(1)}, bf16[512,768]{1,0:T(8,128)(2,1)S(1)}, bf16[256,768]{1,0:T(8,128)(2,1)S(1)...) custom-call(s32[1,8]{1,0:T(1,128)S(1)} %copy-done.10, ...), custom_call_target="tpu_custom_call" | custom-call | tf_op jit(solution)/shard_map/middle/pallas_call | solution.py:428
  113.8 7.7 %collective-permute-done.41 = bf16[96,768]{1,0:T(8,128)(2,1)S(1)} collective-permute-done((bf16[96,768]{1,0:T(8,128)(2,1)S(1)}, bf16[96,768]{1,0:T(8,128)(2,1)S(1)}, u32[]{:S(2)}, u32[]{:S(2)}) %collective-permute-start.41) | collective-permute-done | bytes 147488 | tf_op jit(solution)/shard_map/ppermute | solution.py:322
  134.8 5.6 %collective-permute-start.17 = (bf16[256,768]{1,0:T(8,128)(2,1)S(1)}, bf16[256,768]{1,0:T(8,128)(2,1)S(1)}, u32[]{:S(2)}, u32[]{:S(2)}) collective-permute-start(bf16[256,768]{1,0:T(8,128)(2,1)S(1)} %get-tuple-element.66), channel_id=1, source_target_pairs={{0,3},{1,2},{2,1},{3,0},{4,7},{5,6},{6,5},{7,4},{8,11},{9,10},{10,... | collective-permute-start | bytes 1179656 | tf_op jit(solution)/shard_map/ppermute | solution.py:219
  141.7 4.1 %collective-permute-start.19 = (bf16[256,768]{1,0:T(8,128)(2,1)S(1)}, bf16[256,768]{1,0:T(8,128)(2,1)S(1)}, u32[]{:S(2)}, u32[]{:S(2)}) collective-permute-start(bf16[256,768]{1,0:T(8,128)(2,1)S(1)} %get-tuple-element.67), channel_id=1, source_target_pairs={{0,6},{1,7},{6,0},{7,1},{8,14},{9,15},{14,8},{15,9},{16,22},{17,23... | collective-permute-start | bytes 1179656 | tf_op jit(solution)/shard_map/ppermute | solution.py:219
  145.8 4.6 %collective-permute-start.21 = (bf16[256,768]{1,0:T(8,128)(2,1)S(1)}, bf16[256,768]{1,0:T(8,128)(2,1)S(1)}, u32[]{:S(2)}, u32[]{:S(2)}) collective-permute-start(bf16[256,768]{1,0:T(8,128)(2,1)S(1)} %get-tuple-element.69), channel_id=1, source_target_pairs={{0,7},{1,6},{6,1},{7,0},{8,15},{9,14},{14,9},{15,8},{16,23},{17,22... | collective-permute-start | bytes 1179656 | tf_op jit(solution)/shard_map/ppermute | solution.py:219
  150.5 3.9 %collective-permute-done.31 = bf16[96,768]{1,0:T(8,128)(2,1)S(1)} collective-permute-done((bf16[96,768]{1,0:T(8,128)(2,1)S(1)}, bf16[96,768]{1,0:T(8,128)(2,1)S(1)}, u32[]{:S(2)}, u32[]{:S(2)}) %collective-permute-start.31) | collective-permute-done | bytes 147488 | tf_op jit(solution)/shard_map/ppermute | solution.py:322
  154.4 20.9 %collective-permute-start.29 = (bf16[96,768]{1,0:T(8,128)(2,1)S(1)}, bf16[96,768]{1,0:T(8,128)(2,1)S(1)}, u32[]{:S(2)}, u32[]{:S(2)}) collective-permute-start(bf16[96,768]{1,0:T(8,128)(2,1)S(1)} %add_convert_fusion.3), channel_id=1, source_target_pairs={{0,2},{1,3},{2,0},{3,1},{4,6},{5,7},{6,4},{7,5},{8,10},{9,11},{10,... | collective-permute-start | bytes 442376 | tf_op jit(solution)/shard_map/ppermute | solution.py:322
  177.9 3.9 %collective-permute-start.46 = (bf16[384,768]{1,0:T(8,128)(2,1)S(1)}, bf16[384,768]{1,0:T(8,128)(2,1)S(1)}, u32[]{:S(2)}, u32[]{:S(2)}) collective-permute-start(bf16[384,768]{1,0:T(8,128)(2,1)S(1)} %shard_map.135.refs_0_), channel_id=1, source_target_pairs={{0,1},{1,0},{2,3},{3,2},{4,5},{5,4},{6,7},{7,6},{8,9},{9,8},{10,11... | collective-permute-start | bytes 1769480 | tf_op jit(solution)/shard_map/ppermute | solution.py:322
  185.1 8.5 %collective-permute-done.32.refs_1_ = bf16[96,768]{1,0:T(8,128)(2,1)S(1)} collective-permute-done((bf16[96,768]{1,0:T(8,128)(2,1)S(1)}, bf16[96,768]{1,0:T(8,128)(2,1)S(1)}, u32[]{:S(2)}, u32[]{:S(2)}) %collective-permute-start.32) | collective-permute-done | bytes 147488 | tf_op jit(solution)/shard_map/ppermute | solution.py:322
  194.8 3.9 %collective-permute-start.24 = (bf16[256,768]{1,0:T(8,128)(2,1)S(1)}, bf16[256,768]{1,0:T(8,128)(2,1)S(1)}, u32[]{:S(2)}, u32[]{:S(2)}) collective-permute-start(bf16[256,768]{1,0:T(8,128)(2,1)S(1)} %get-tuple-element.72), channel_id=1, source_target_pairs={{0,24},{8,0},{16,8},{24,16},{1,25},{9,1},{17,9},{25,17},{2,26},{10... | collective-permute-start | bytes 1179656 | tf_op jit(solution)/shard_map/ppermute | solution.py:253
  202.1 11.5 %collective-permute-done.23.rest_8_ = bf16[256,768]{1,0:T(8,128)(2,1)S(1)} collective-permute-done((bf16[256,768]{1,0:T(8,128)(2,1)S(1)}, bf16[256,768]{1,0:T(8,128)(2,1)S(1)}, u32[]{:S(2)}, u32[]{:S(2)}) %collective-permute-start.23) | collective-permute-done | bytes 393248 | tf_op jit(solution)/shard_map/ppermute | solution.py:253
  221.1 8.5 %sweep.3.base = f32[2,256,768]{2,1,0:T(8,128)S(1)} custom-call(s32[1,24]{1,0:T(1,128)S(1)} %copy-done.11, s32[1,24]{1,0:T(1,128)S(1)} %copy-done.9, s32[1]{0:T(128)S(6)} %copy.18.block_count, s32[1,4,1]{2,1,0:T(4,128)S(1)} %copy.17.send_member, s32[1,8]{1,0:T(1,128)S(1)} %collective-permute-done.far_table, bf16[512,768]{1,0:T(8,128)(2,1)S(1)} %get-tuple-element.62.back, ...), custom_call_target="tpu_custom_call" | custom-call | tf_op jit(solution)/shard_map/sweep/pallas_call | solution.py:394
  229.9 8.2 %collective-permute-done.50.rest_3_ = bf16[256,768]{1,0:T(8,128)(2,1)S(1)} collective-permute-done((bf16[256,768]{1,0:T(8,128)(2,1)S(1)}, bf16[256,768]{1,0:T(8,128)(2,1)S(1)}, u32[]{:S(2)}, u32[]{:S(2)}) %collective-permute-start.50) | collective-permute-done | bytes 393248 | tf_op jit(solution)/shard_map/ppermute | solution.py:219
  238.1 3.6 %last.1 = (bf16[512,768]{1,0:T(8,128)(2,1)}, f32[768,768]{1,0:T(8,128)}) custom-call(s32[1,24]{1,0:T(1,128)S(1)} %copy-done.9, s32[1,8]{1,0:T(1,128)S(1)} %collective-permute-done.far_table, f32[2,256,768]{2,1,0:T(8,128)S(1)} %sweep.3.base, bf16[384,768]{1,0:T(8,128)(2,1)S(1)} %shard_map.132.own_half, ...), custom_call_target="tpu_custom_call" | custom-call | tf_op jit(solution)/shard_map/last/pallas_call | solution.py:449
  (122 shorter events, 69.6 us)
Async XLA Ops:
  10.2 29.3 %collective-permute-start.4 = (bf16[512,768]{1,0:T(8,128)(2,1)S(1)}, bf16[512,768]{1,0:T(8,128)(2,1)S(1)}, u32[]{:S(2)}, u32[]{:S(2)}) collective-permute-start(bf16[512,768]{1,0:T(8,128)(2,1)S(1)} %get-tuple-element.48.back), channel_id=1, source_target_pairs={{2,4},{3,5},{4,2},{5,3},{10,12},{11,13},{12,10},{13,11},{18,20},{1... | collective-permute-start | bytes 2359304 | tf_op jit(solution)/shard_map/ppermute | solution.py:219
  10.9 22.4 %collective-permute-start.1 = (bf16[256,768]{1,0:T(8,128)(2,1)S(1)}, bf16[256,768]{1,0:T(8,128)(2,1)S(1)}, u32[]{:S(2)}, u32[]{:S(2)}) collective-permute-start(bf16[256,768]{1,0:T(8,128)(2,1)S(1)} %get-tuple-element.49), channel_id=1, source_target_pairs={{0,1},{1,0},{2,3},{3,2},{4,5},{5,4},{6,7},{7,6},{8,9},{9,8},{10,11... | collective-permute-start | bytes 1179656 | tf_op jit(solution)/shard_map/ppermute | solution.py:219
  11.6 25.8 %collective-permute-start.2 = (bf16[256,768]{1,0:T(8,128)(2,1)S(1)}, bf16[256,768]{1,0:T(8,128)(2,1)S(1)}, u32[]{:S(2)}, u32[]{:S(2)}) collective-permute-start(bf16[256,768]{1,0:T(8,128)(2,1)S(1)} %get-tuple-element.50), channel_id=1, source_target_pairs={{0,2},{1,3},{2,0},{3,1},{4,6},{5,7},{6,4},{7,5},{8,10},{9,11},{10,... | collective-permute-start | bytes 1179656 | tf_op jit(solution)/shard_map/ppermute | solution.py:219
  17.0 45.8 %collective-permute-start.36 = (bf16[384,768]{1,0:T(8,128)(2,1)S(1)}, bf16[384,768]{1,0:T(8,128)(2,1)S(1)}, u32[]{:S(2)}, u32[]{:S(2)}) collective-permute-start(bf16[384,768]{1,0:T(8,128)(2,1)S(1)} %get-tuple-element.82), channel_id=1, source_target_pairs={{0,1},{1,0},{2,3},{3,2},{4,5},{5,4},{6,7},{7,6},{8,9},{9,8},{10,11... | collective-permute-start | bytes 1769480 | tf_op jit(solution)/shard_map/ppermute | solution.py:322
  33.3 20.0 %collective-permute-start.5 = (bf16[256,768]{1,0:T(8,128)(2,1)S(1)}, bf16[256,768]{1,0:T(8,128)(2,1)S(1)}, u32[]{:S(2)}, u32[]{:S(2)}) collective-permute-start(bf16[256,768]{1,0:T(8,128)(2,1)S(1)} %get-tuple-element.52), channel_id=1, source_target_pairs={{0,6},{1,7},{6,0},{7,1},{8,14},{9,15},{14,8},{15,9},{16,22},{17,23... | collective-permute-start | bytes 1179656 | tf_op jit(solution)/shard_map/ppermute | solution.py:219
  37.4 22.8 %collective-permute-start.7 = (bf16[256,768]{1,0:T(8,128)(2,1)S(1)}, bf16[256,768]{1,0:T(8,128)(2,1)S(1)}, u32[]{:S(2)}, u32[]{:S(2)}) collective-permute-start(bf16[256,768]{1,0:T(8,128)(2,1)S(1)} %get-tuple-element.54), channel_id=1, source_target_pairs={{0,7},{1,6},{6,1},{7,0},{8,15},{9,14},{14,9},{15,8},{16,23},{17,22... | collective-permute-start | bytes 1179656 | tf_op jit(solution)/shard_map/ppermute | solution.py:219
  39.5 22.0 %collective-permute-start.8 = (bf16[256,768]{1,0:T(8,128)(2,1)S(1)}, bf16[256,768]{1,0:T(8,128)(2,1)S(1)}, u32[]{:S(2)}, u32[]{:S(2)}) collective-permute-start(bf16[256,768]{1,0:T(8,128)(2,1)S(1)} %get-tuple-element.55), channel_id=1, source_target_pairs={{0,8},{8,16},{16,24},{24,0},{1,9},{9,17},{17,25},{25,1},{2,10},{10... | collective-permute-start | bytes 1179656 | tf_op jit(solution)/shard_map/ppermute | solution.py:253
  42.2 21.4 %collective-permute-start.9 = (bf16[256,768]{1,0:T(8,128)(2,1)S(1)}, bf16[256,768]{1,0:T(8,128)(2,1)S(1)}, u32[]{:S(2)}, u32[]{:S(2)}) collective-permute-start(bf16[256,768]{1,0:T(8,128)(2,1)S(1)} %get-tuple-element.56), channel_id=1, source_target_pairs={{0,16},{8,24},{16,0},{24,8},{1,17},{9,25},{17,1},{25,9},{2,18},{10... | collective-permute-start | bytes 1179656 | tf_op jit(solution)/shard_map/ppermute | solution.py:253
  63.7 43.2 %collective-permute-start.39 = (bf16[96,768]{1,0:T(8,128)(2,1)S(1)}, bf16[96,768]{1,0:T(8,128)(2,1)S(1)}, u32[]{:S(2)}, u32[]{:S(2)}) collective-permute-start(bf16[96,768]{1,0:T(8,128)(2,1)S(1)} %get-tuple-element.86), channel_id=1, source_target_pairs={{0,24},{8,16},{16,8},{24,0},{1,25},{9,17},{17,9},{25,1},{2,26},{10... | collective-permute-start | bytes 442376 | tf_op jit(solution)/shard_map/ppermute | solution.py:322
  64.9 41.9 %collective-permute-start.38 = (bf16[96,768]{1,0:T(8,128)(2,1)S(1)}, bf16[96,768]{1,0:T(8,128)(2,1)S(1)}, u32[]{:S(2)}, u32[]{:S(2)}) collective-permute-start(bf16[96,768]{1,0:T(8,128)(2,1)S(1)} %get-tuple-element.85), channel_id=1, source_target_pairs={{0,16},{8,24},{16,0},{24,8},{1,17},{9,25},{17,1},{25,9},{2,18},{10... | collective-permute-start | bytes 442376 | tf_op jit(solution)/shard_map/ppermute | solution.py:322
  68.9 38.0 %collective-permute-start.37 = (bf16[96,768]{1,0:T(8,128)(2,1)S(1)}, bf16[96,768]{1,0:T(8,128)(2,1)S(1)}, u32[]{:S(2)}, u32[]{:S(2)}) collective-permute-start(bf16[96,768]{1,0:T(8,128)(2,1)S(1)} %get-tuple-element.84), channel_id=1, source_target_pairs={{0,8},{8,0},{16,24},{24,16},{1,9},{9,1},{17,25},{25,17},{2,10},{10... | collective-permute-start | bytes 442376 | tf_op jit(solution)/shard_map/ppermute | solution.py:322
  78.6 21.0 %collective-permute-start.14 = (bf16[256,768]{1,0:T(8,128)(2,1)S(1)}, bf16[256,768]{1,0:T(8,128)(2,1)S(1)}, u32[]{:S(2)}, u32[]{:S(2)}) collective-permute-start(bf16[256,768]{1,0:T(8,128)(2,1)S(1)} %get-tuple-element.61), channel_id=1, source_target_pairs={{2,1},{3,0},{4,7},{5,6},{10,9},{11,8},{12,15},{13,14},{18,17},{19,... | collective-permute-start | bytes 1179656 | tf_op jit(solution)/shard_map/ppermute | solution.py:219
  130.3 54.4 %collective-permute-start.18 = (bf16[512,768]{1,0:T(8,128)(2,1)S(1)}, bf16[512,768]{1,0:T(8,128)(2,1)S(1)}, u32[]{:S(2)}, u32[]{:S(2)}) collective-permute-start(bf16[512,768]{1,0:T(8,128)(2,1)S(1)} %get-tuple-element.62.back), channel_id=1, source_target_pairs={{2,4},{3,5},{4,2},{5,3},{10,12},{11,13},{12,10},{13,11},{18,20},{1... | collective-permute-start | bytes 2359304 | tf_op jit(solution)/shard_map/ppermute | solution.py:219
  141.7 40.7 %collective-permute-start.19 = (bf16[256,768]{1,0:T(8,128)(2,1)S(1)}, bf16[256,768]{1,0:T(8,128)(2,1)S(1)}, u32[]{:S(2)}, u32[]{:S(2)}) collective-permute-start(bf16[256,768]{1,0:T(8,128)(2,1)S(1)} %get-tuple-element.67), channel_id=1, source_target_pairs={{0,6},{1,7},{6,0},{7,1},{8,14},{9,15},{14,8},{15,9},{16,22},{17,23... | collective-permute-start | bytes 1179656 | tf_op jit(solution)/shard_map/ppermute | solution.py:219
  145.8 37.6 %collective-permute-start.21 = (bf16[256,768]{1,0:T(8,128)(2,1)S(1)}, bf16[256,768]{1,0:T(8,128)(2,1)S(1)}, u32[]{:S(2)}, u32[]{:S(2)}) collective-permute-start(bf16[256,768]{1,0:T(8,128)(2,1)S(1)} %get-tuple-element.69), channel_id=1, source_target_pairs={{0,7},{1,6},{6,1},{7,0},{8,15},{9,14},{14,9},{15,8},{16,23},{17,22... | collective-permute-start | bytes 1179656 | tf_op jit(solution)/shard_map/ppermute | solution.py:219
  150.4 27.5 %collective-permute-start.30 = (bf16[96,768]{1,0:T(8,128)(2,1)S(1)}, bf16[96,768]{1,0:T(8,128)(2,1)S(1)}, u32[]{:S(2)}, u32[]{:S(2)}) collective-permute-start(bf16[96,768]{1,0:T(8,128)(2,1)S(1)} %add_convert_fusion.3), channel_id=1, source_target_pairs={{0,4},{1,5},{2,6},{3,7},{4,0},{5,1},{6,2},{7,3},{8,12},{9,13},{10,... | collective-permute-start | bytes 442376 | tf_op jit(solution)/shard_map/ppermute | solution.py:322
  154.4 27.4 %collective-permute-start.29 = (bf16[96,768]{1,0:T(8,128)(2,1)S(1)}, bf16[96,768]{1,0:T(8,128)(2,1)S(1)}, u32[]{:S(2)}, u32[]{:S(2)}) collective-permute-start(bf16[96,768]{1,0:T(8,128)(2,1)S(1)} %add_convert_fusion.3), channel_id=1, source_target_pairs={{0,2},{1,3},{2,0},{3,1},{4,6},{5,7},{6,4},{7,5},{8,10},{9,11},{10,... | collective-permute-start | bytes 442376 | tf_op jit(solution)/shard_map/ppermute | solution.py:322
  177.9 39.0 %collective-permute-start.46 = (bf16[384,768]{1,0:T(8,128)(2,1)S(1)}, bf16[384,768]{1,0:T(8,128)(2,1)S(1)}, u32[]{:S(2)}, u32[]{:S(2)}) collective-permute-start(bf16[384,768]{1,0:T(8,128)(2,1)S(1)} %shard_map.135.refs_0_), channel_id=1, source_target_pairs={{0,1},{1,0},{2,3},{3,2},{4,5},{5,4},{6,7},{7,6},{8,9},{9,8},{10,11... | collective-permute-start | bytes 1769480 | tf_op jit(solution)/shard_map/ppermute | solution.py:322
  181.8 18.8 %collective-permute-start.22 = (bf16[256,768]{1,0:T(8,128)(2,1)S(1)}, bf16[256,768]{1,0:T(8,128)(2,1)S(1)}, u32[]{:S(2)}, u32[]{:S(2)}) collective-permute-start(bf16[256,768]{1,0:T(8,128)(2,1)S(1)} %get-tuple-element.70), channel_id=1, source_target_pairs={{0,8},{8,16},{16,24},{24,0},{1,9},{9,17},{17,25},{25,1},{2,10},{10... | collective-permute-start | bytes 1179656 | tf_op jit(solution)/shard_map/ppermute | solution.py:253
  193.5 20.1 %collective-permute-start.23 = (bf16[256,768]{1,0:T(8,128)(2,1)S(1)}, bf16[256,768]{1,0:T(8,128)(2,1)S(1)}, u32[]{:S(2)}, u32[]{:S(2)}) collective-permute-start(bf16[256,768]{1,0:T(8,128)(2,1)S(1)} %get-tuple-element.71), channel_id=1, source_target_pairs={{0,16},{8,24},{16,0},{24,8},{1,17},{9,25},{17,1},{25,9},{2,18},{10... | collective-permute-start | bytes 1179656 | tf_op jit(solution)/shard_map/ppermute | solution.py:253
  194.8 20.1 %collective-permute-start.24 = (bf16[256,768]{1,0:T(8,128)(2,1)S(1)}, bf16[256,768]{1,0:T(8,128)(2,1)S(1)}, u32[]{:S(2)}, u32[]{:S(2)}) collective-permute-start(bf16[256,768]{1,0:T(8,128)(2,1)S(1)} %get-tuple-element.72), channel_id=1, source_target_pairs={{0,24},{8,0},{16,8},{24,16},{1,25},{9,1},{17,9},{25,17},{2,26},{10... | collective-permute-start | bytes 1179656 | tf_op jit(solution)/shard_map/ppermute | solution.py:253
  199.9 18.3 %collective-permute-start.20 = (bf16[256,768]{1,0:T(8,128)(2,1)S(1)}, bf16[256,768]{1,0:T(8,128)(2,1)S(1)}, u32[]{:S(2)}, u32[]{:S(2)}) collective-permute-start(bf16[256,768]{1,0:T(8,128)(2,1)S(1)} %get-tuple-element.68), channel_id=1, source_target_pairs={{2,3},{3,2},{4,5},{5,4},{10,11},{11,10},{12,13},{13,12},{18,19},{1... | collective-permute-start | bytes 1179656 | tf_op jit(solution)/shard_map/ppermute | solution.py:219
  200.6 37.4 %collective-permute-start.35 = (bf16[384,768]{1,0:T(8,128)(2,1)S(1)}, bf16[384,768]{1,0:T(8,128)(2,1)S(1)}, u32[]{:S(2)}, u32[]{:S(2)}) collective-permute-start(bf16[384,768]{1,0:T(8,128)(2,1)S(1)} %shard_map.132.own_half), channel_id=1, source_target_pairs={{0,1},{1,0},{2,3},{3,2},{4,5},{5,4},{6,7},{7,6},{8,9},{9,8},{10,11... | collective-permute-start | bytes 1769480 | tf_op jit(solution)/shard_map/ppermute | solution.py:322
  218.2 19.9 %collective-permute-start.50 = (bf16[256,768]{1,0:T(8,128)(2,1)S(1)}, bf16[256,768]{1,0:T(8,128)(2,1)S(1)}, u32[]{:S(2)}, u32[]{:S(2)}) collective-permute-start(bf16[256,768]{1,0:T(8,128)(2,1)S(1)} %get-tuple-element.90), channel_id=1, source_target_pairs={{2,1},{3,0},{4,7},{5,6},{10,9},{11,8},{12,15},{13,14},{18,17},{19,... | collective-permute-start | bytes 1179656 | tf_op jit(solution)/shard_map/ppermute | solution.py:219
  (39 other events, 492.3 us)
